TPU v7x, 512 devices: a whole 4x4x16 slice. The times are simulated.
512 devices in a mesh: sub: 8 (over z_lo), gate: 64 (over z_hi, x, y, core).
Axes of the slice: x: 4, y: 4, z: 16 (z_hi: 2, z_lo: 8; z = z_hi * 8 + z_lo), core: 2. Of those that a mesh axis runs over, the one named last changes fastest.
Arguments:
- raw_echo: bfloat16 [2, 4096, 16384], P(None, ('sub', 'gate')), may hold values from -6 to 6
- delays: int32 [4096], P(('sub', 'gate')), may hold values from 0 to 64
Outputs:
- image: bfloat16 [2, 2048, 16384], P(None, 'sub', 'gate')
All inputs are finite; a program needn't handle non-finite values.
Results may differ from a plain program's by a relative error of at most 0.009.
Values may be sent and summed in bfloat16 or wider, within the bound.
A program may use at most 64 MiB of HBM per device.

v0:
```python
import math

import jax
import jax.numpy as jnp
from jax import lax
from jax.sharding import PartitionSpec as P

RADIX = 128
SAMPLES = 16384
ANGLES = 256
DELAY_MAX = 64


TWO_PI = 2.0 * math.pi


def partner(array, axis, apart):
    return lax.ppermute(array, axis, [(i, i ^ 1 << apart) for i in range(lax.axis_size(axis))])


def complex_blocks(real_part, imag_part):
    upper = jnp.stack([real_part, -imag_part], axis=1)
    lower = jnp.stack([imag_part, real_part], axis=1)
    return jnp.stack([upper, lower], axis=0).astype(jnp.bfloat16)


def dft_blocks(order):
    counter = jnp.arange(order, dtype=jnp.int32)
    product = counter[:, None] * counter[None, :] % order
    phases = -TWO_PI / order * product.astype(jnp.float32)
    factor = 1.0 / math.sqrt(order)
    return complex_blocks(jnp.cos(phases) * factor, jnp.sin(phases) * factor)


def steer_blocks(beam_count, pulse_count):
    beam_index = jnp.arange(beam_count, dtype=jnp.int32)
    pulse_index = jnp.arange(pulse_count, dtype=jnp.int32)
    modulus = 16 * beam_count
    product = (
        (2 * beam_index[:, None] - beam_count + 1)
        * (2 * pulse_index[None, :] - pulse_count + 1)
        % modulus
    )
    phases = -TWO_PI / modulus * product.astype(jnp.float32)
    factor = 1.0 / math.sqrt(pulse_count)
    return complex_blocks(jnp.cos(phases) * factor, jnp.sin(phases) * factor)


def interp_table(beam_count):
    half_count = beam_count // 2
    targets = jnp.arange(beam_count, dtype=jnp.float32)
    sources = jnp.arange(half_count, dtype=jnp.float32)
    distance = targets[:, None] * 0.5 - 0.25 - sources[None, :]
    taper = jnp.where(jnp.abs(distance) < 4.0, 0.5 + 0.5 * jnp.cos(math.pi * distance / 4.0), 0.0)
    return (jnp.sinc(distance) * taper).astype(jnp.bfloat16)


def rotation(center, numerator, depth, gate_pos):
    modulus = ANGLES * 2 ** (depth + 3)
    turns = jnp.mod(center * numerator, modulus).astype(jnp.float32) / modulus
    center_sq = (center * center).astype(jnp.float32)
    near_term = center_sq / (16.0 * (SAMPLES + gate_pos))
    phases = -TWO_PI * turns[:, None] - TWO_PI / (4 * ANGLES) * near_term[None, :]
    factor = 1.0 / math.sqrt(2.0)
    return (jnp.cos(phases) * factor, jnp.sin(phases) * factor)


def range_compress(raw_echo, delays):
    pulse_count = raw_echo.shape[1]
    dft_table = dft_blocks(RADIX)
    samples_grid = raw_echo.reshape(2, pulse_count, RADIX, RADIX)
    section_one = jnp.einsum(
        "akcn,cpnm->apkm", dft_table, samples_grid, preferred_element_type=jnp.float32
    )
    counter = jnp.arange(RADIX, dtype=jnp.int32)
    phases = -TWO_PI / SAMPLES * (counter[:, None] * counter[None, :]).astype(jnp.float32)
    cosine = jnp.cos(phases)
    sine_part = jnp.sin(phases)
    twisted = jnp.stack(
        [
            section_one[0] * cosine - section_one[1] * sine_part,
            section_one[0] * sine_part + section_one[1] * cosine,
        ]
    ).astype(jnp.bfloat16)
    spectrum = jnp.einsum("akcn,cpjn->apkj", dft_table, twisted, preferred_element_type=jnp.float32)
    rounded = spectrum.reshape(2, pulse_count, SAMPLES).astype(jnp.bfloat16)
    padded = jnp.pad(rounded, ((0, 0), (0, 0), (0, DELAY_MAX)))

    def shift_row(pulse_row, start):
        return lax.dynamic_slice_in_dim(pulse_row, start, SAMPLES, axis=1)

    return jax.vmap(shift_row, in_axes=(1, 0), out_axes=1)(padded, delays)


def merge_pair(child, depth, sub_index, sector, gate_pos, sub_pulses):
    half_count = ANGLES // 2
    side_bit = sub_index // 2 ** (depth - 1) % 2
    partner_full = partner(child, "sub", depth - 1)
    partner_half = lax.dynamic_slice_in_dim(partner_full, side_bit * half_count, half_count, axis=1)
    own_half = lax.dynamic_slice_in_dim(child, side_bit * half_count, half_count, axis=1)
    paired = jnp.stack([own_half, partner_half], axis=0)
    moved = jnp.einsum(
        "jh,kchg->kcjg", interp_table(ANGLES), paired, preferred_element_type=jnp.float32
    )
    sector_next = 2 * sector + side_bit
    row_index = sector_next * ANGLES + jnp.arange(ANGLES, dtype=jnp.int32)
    numerator = 2 * row_index + 1 - ANGLES * 2**depth
    offset = sub_pulses * 2 ** (depth - 1) // 2
    own_center = (2 * side_bit - 1) * offset
    total_real = jnp.zeros((ANGLES, child.shape[-1]), jnp.float32)
    total_imag = jnp.zeros((ANGLES, child.shape[-1]), jnp.float32)
    for member in range(2):
        center = own_center * (1 - 2 * member)
        cosine, sine_part = rotation(center, numerator, depth, gate_pos)
        total_real = total_real + cosine * moved[member, 0] - sine_part * moved[member, 1]
        total_imag = total_imag + sine_part * moved[member, 0] + cosine * moved[member, 1]
    merged = jnp.stack([total_real, total_imag], axis=0).astype(jnp.bfloat16)
    return (merged, sector_next)


def per_device(raw_echo, delays):
    gate_count = lax.axis_size("gate")
    sub_count = lax.axis_size("sub")
    pulse_count = raw_echo.shape[1]
    sub_pulses = pulse_count * gate_count
    gate_width = SAMPLES // gate_count
    depth_count = sub_count.bit_length() - 1
    compressed = range_compress(raw_echo, delays)
    steering = steer_blocks(ANGLES, sub_pulses)
    layout = compressed.reshape(2, pulse_count, gate_count, gate_width)
    received = lax.all_to_all(layout, "gate", split_axis=2, concat_axis=1, tiled=True)
    flat_block = received.reshape(2, received.shape[1], received.shape[3])
    current = jnp.einsum(
        "akcm,cmg->akg", steering, flat_block, preferred_element_type=jnp.float32
    ).astype(jnp.bfloat16)
    gate_pos = (
        lax.axis_index("gate") * gate_width + jnp.arange(gate_width, dtype=jnp.int32)
    ).astype(jnp.float32)
    sub_index = lax.axis_index("sub")
    sector = jnp.zeros((), jnp.int32)
    for depth in range(1, depth_count + 1):
        current, sector = merge_pair(current, depth, sub_index, sector, gate_pos, sub_pulses)
    return current


def solution(mesh):
    placed = (P(None, ("sub", "gate"), None), P(("sub", "gate")))
    return jax.shard_map(
        per_device, mesh=mesh, in_specs=placed, out_specs=P(None, "sub", "gate"), check_vma=False
    )
```

profile of v0, /device:TPU:1, one launch (start us, length us, event | category | flops | bytes accessed | tf_op | source)
XLA Modules:
  0.0 148.3 jit_solution(8874161268157996369)
XLA Ops:
  0.0 0.3 negate_convert_fusion.1
  0.3 0.3 fusion.128
  0.6 0.3 fusion.123
  0.8 1.3 convolution_bitcast_fusion.4
  2.2 0.1 subtract_convert_fusion
  2.3 0.3 fusion.1
  2.7 0.3 copy.25
  3.0 0.2 convert_element_type.184
  3.2 0.0 copy-start
  3.3 0.4 copy.26
  3.7 0.2 copy-done
  3.9 16.9 %while.1 = (s32[]{:T(128)}, bf16[8,2,16448]{2,1,0:T(2,128)(2,1)S(1)}, s32[8,3]{0,1:T(4,128)S(1)}, bf16[8,2,16384]{2,1,0:T(2,128)(2,1)S(1)}, s32[]{:T(128)}) while((s32[]{:T(128)}, bf16[8,2,16448]{2,1,0:T(2,128)(2,1)S(1)}, s32[8,3]{0,1:T(4,128)S(1)}, bf16[8,2,16384]{2,1,0:T(2,128)(2,1)S(1)}, s32[]{:T(128)}) %tuple.36), condition=%wide.while_cond, body=%wide.while_body.sunk | while | flops 2 | bytes 131189 | solution.py:90
  3.9 0.1 constant_dynamic-slice_fusion.2
  4.0 0.6 fusion.196
  4.6 1.4 dynamic-slice_dynamic-update-slice_fusion.2
  6.0 0.1 constant_dynamic-slice_fusion.2
  6.1 0.6 fusion.196
  6.7 1.4 dynamic-slice_dynamic-update-slice_fusion.2
  8.1 0.1 constant_dynamic-slice_fusion.2
  8.2 0.6 fusion.196
  8.8 1.4 dynamic-slice_dynamic-update-slice_fusion.2
  10.3 0.1 constant_dynamic-slice_fusion.2
  10.3 0.6 fusion.196
  10.9 1.4 dynamic-slice_dynamic-update-slice_fusion.2
  12.4 0.1 constant_dynamic-slice_fusion.2
  12.4 0.6 fusion.196
  13.0 1.4 dynamic-slice_dynamic-update-slice_fusion.2
  14.5 0.1 constant_dynamic-slice_fusion.2
  14.5 0.6 fusion.196
  15.1 1.4 dynamic-slice_dynamic-update-slice_fusion.2
  16.6 0.1 constant_dynamic-slice_fusion.2
  16.7 0.6 fusion.196
  17.3 1.4 dynamic-slice_dynamic-update-slice_fusion.2
  18.7 0.1 constant_dynamic-slice_fusion.2
  18.8 0.6 fusion.196
  19.4 1.4 dynamic-slice_dynamic-update-slice_fusion.2
  20.8 0.3 reshape.1353
  21.1 1.1 copy.28
  22.2 22.2 %all-to-all-start = ((bf16[2,8,64,256]{3,1,0,2:T(8,128)(2,1)}), bf16[2,8,64,256]{3,1,0,2:T(8,128)(2,1)S(1)}, u32[]{:S(2)}, u32[]{:S(2)}) async-start(bf16[2,8,64,256]{3,1,0,2:T(8,128)(2,1)} %copy.28), calls=%async_computation | async-start | bytes 1048576 | tf_op jit(solution)/shard_map/all_to_all | solution.py:131
  44.5 2.5 %negate_convert_fusion = (bf16[256,1,512]{2,0,1:T(8,128)(2,1)S(1)}, bf16[256,1,512]{2,0,1:T(8,128)(2,1)S(1)}, bf16[256,1,512]{2,0,1:T(8,128)(2,1)S(1)}) fusion(s32[512]{0:T(512)S(1)} %multiply_add_fusion.1, s32[256]{0:T(256)S(1)} %multiply_add_fusion.3), kind=kLoop, calls=%fused_computation.33 | loop fusion | flops 2621440 | bytes 789504 | tf_op jit(solution)/shard_map/convert.23
  47.0 0.1 maximum_bitcast_fusion
  47.1 18.5 %all-to-all-done = bf16[2,8,64,256]{3,1,0,2:T(8,128)(2,1)S(1)} async-done(((bf16[2,8,64,256]{3,1,0,2:T(8,128)(2,1)}), bf16[2,8,64,256]{3,1,0,2:T(8,128)(2,1)S(1)}, u32[]{:S(2)}, u32[]{:S(2)}) %all-to-all-start) | async-done | bytes 524320 | tf_op jit(solution)/shard_map/all_to_all | solution.py:131
  65.7 0.4 fusion.2
  66.1 19.2 %collective-permute-start = (bf16[2,256,256]{2,1,0:T(8,128)(2,1)S(1)}, bf16[2,256,256]{2,1,0:T(8,128)(2,1)S(1)}, u32[]{:S(2)}, u32[]{:S(2)}) collective-permute-start(bf16[2,256,256]{2,1,0:T(8,128)(2,1)S(1)} %fusion.2), channel_id=1, source_target_pairs={{0,64},{64,0},{128,192},{192,128},{256,320},{320,256},{384,448},{4... | collective-permute-start | bytes 786440 | tf_op jit(solution)/shard_map/ppermute | solution.py:18
  85.4 0.1 copy.30
  85.6 6.3 %collective-permute-done = bf16[2,256,256]{2,1,0:T(8,128)(2,1)S(1)} collective-permute-done((bf16[2,256,256]{2,1,0:T(8,128)(2,1)S(1)}, bf16[2,256,256]{2,1,0:T(8,128)(2,1)S(1)}, u32[]{:S(2)}, u32[]{:S(2)}) %collective-permute-start) | collective-permute-done | bytes 262176 | tf_op jit(solution)/shard_map/ppermute | solution.py:18
  91.9 0.1 copy.31
  92.0 1.0 convolution_bitcast_fusion.2
  92.9 2.4 %fusion.49 = (bf16[1,256,256]{1,2,0:T(8,128)(2,1)S(1)}, bf16[1,256,256]{1,2,0:T(8,128)(2,1)S(1)}) fusion(f32[2,2,256,256]{2,3,1,0:T(8,128)S(1)} %convolution_bitcast_fusion.2, f32[256]{0:T(256)S(1)} %get-tuple-element.56, f32[256]{0:T(256)S(1)} %divide_multiply_fusion, f32[256]{0:T(256)S(1)} %get-tuple-element.55), kind=kLoop, calls=%fused_computation.89 | loop fusion | flops 1441792 | bytes 1313792 | tf_op jit(solution)/shard_map/convert.4
  95.4 1.9 %collective-permute-start.1 = (bf16[2,256,256]{1,2,0:T(8,128)(2,1)S(1)}, bf16[2,256,256]{1,2,0:T(8,128)(2,1)S(1)}, u32[]{:S(2)}, u32[]{:S(2)}) collective-permute-start(bf16[2,256,256]{1,2,0:T(8,128)(2,1)S(1)} %pad_maximum_fusion), channel_id=1, source_target_pairs={{0,128},{64,192},{128,0},{192,64},{256,384},{320,448},{384,256},{4... | collective-permute-start | bytes 786440 | tf_op jit(solution)/shard_map/ppermute | solution.py:18
  97.4 13.7 %collective-permute-done.1 = bf16[2,256,256]{1,2,0:T(8,128)(2,1)S(1)} collective-permute-done((bf16[2,256,256]{1,2,0:T(8,128)(2,1)S(1)}, bf16[2,256,256]{1,2,0:T(8,128)(2,1)S(1)}, u32[]{:S(2)}, u32[]{:S(2)}) %collective-permute-start.1) | collective-permute-done | bytes 262176 | tf_op jit(solution)/shard_map/ppermute | solution.py:18
  111.2 1.0 convolution_bitcast_fusion.1
  112.1 2.4 %fusion.35 = (bf16[1,256,256]{1,2,0:T(8,128)(2,1)S(1)}, bf16[1,256,256]{1,2,0:T(8,128)(2,1)S(1)}) fusion(f32[2,2,256,256]{2,3,1,0:T(8,128)S(1)} %convolution_bitcast_fusion.1, f32[256]{0:T(256)S(1)} %get-tuple-element.54, f32[256]{0:T(256)S(1)} %divide_multiply_fusion.1, f32[256]{0:T(256)S(1)} %get-tuple-element.53), kind=kLoop, calls=%fused_computation.75 | loop fusion | flops 1441792 | bytes 1313792 | tf_op jit(solution)/shard_map/convert.2
  114.6 4.1 %collective-permute-start.2 = (bf16[2,256,256]{1,2,0:T(8,128)(2,1)S(1)}, bf16[2,256,256]{1,2,0:T(8,128)(2,1)S(1)}, u32[]{:S(2)}, u32[]{:S(2)}) collective-permute-start(bf16[2,256,256]{1,2,0:T(8,128)(2,1)S(1)} %pad_maximum_fusion.1), channel_id=1, source_target_pairs={{0,256},{64,320},{128,384},{192,448},{256,0},{320,64},{384,128},{4... | collective-permute-start | bytes 786440 | tf_op jit(solution)/shard_map/ppermute | solution.py:18
  118.7 25.3 %collective-permute-done.2 = bf16[2,256,256]{1,2,0:T(8,128)(2,1)S(1)} collective-permute-done((bf16[2,256,256]{1,2,0:T(8,128)(2,1)S(1)}, bf16[2,256,256]{1,2,0:T(8,128)(2,1)S(1)}, u32[]{:S(2)}, u32[]{:S(2)}) %collective-permute-start.2) | collective-permute-done | bytes 262176 | tf_op jit(solution)/shard_map/ppermute | solution.py:18
  144.0 0.9 convolution_bitcast_fusion
  145.0 2.4 %fusion.21 = (bf16[1,256,256]{1,2,0:T(8,128)(2,1)S(1)}, bf16[1,256,256]{1,2,0:T(8,128)(2,1)S(1)}) fusion(f32[2,2,256,256]{2,3,1,0:T(8,128)S(1)} %convolution_bitcast_fusion, f32[256]{0:T(256)S(1)} %get-tuple-element.52, f32[256]{0:T(256)S(1)} %divide_multiply_fusion.2, f32[256]{0:T(256)S(1)} %get-tuple-element.51), kind=kLoop, calls=%fused_computation.61 | loop fusion | flops 1441792 | bytes 1313792 | tf_op jit(solution)/shard_map/convert
  147.4 0.8 copy.32
  (24 shorter events, 0.3 us)
Async XLA Ops:
  3.2 0.7 copy-start
  22.2 43.5 %all-to-all-start = ((bf16[2,8,64,256]{3,1,0,2:T(8,128)(2,1)}), bf16[2,8,64,256]{3,1,0,2:T(8,128)(2,1)S(1)}, u32[]{:S(2)}, u32[]{:S(2)}) async-start(bf16[2,8,64,256]{3,1,0,2:T(8,128)(2,1)} %copy.28), calls=%async_computation | async-start | bytes 1048576 | tf_op jit(solution)/shard_map/all_to_all | solution.py:131
  66.1 25.7 %collective-permute-start = (bf16[2,256,256]{2,1,0:T(8,128)(2,1)S(1)}, bf16[2,256,256]{2,1,0:T(8,128)(2,1)S(1)}, u32[]{:S(2)}, u32[]{:S(2)}) collective-permute-start(bf16[2,256,256]{2,1,0:T(8,128)(2,1)S(1)} %fusion.2), channel_id=1, source_target_pairs={{0,64},{64,0},{128,192},{192,128},{256,320},{320,256},{384,448},{4... | collective-permute-start | bytes 786440 | tf_op jit(solution)/shard_map/ppermute | solution.py:18
  95.4 15.8 %collective-permute-start.1 = (bf16[2,256,256]{1,2,0:T(8,128)(2,1)S(1)}, bf16[2,256,256]{1,2,0:T(8,128)(2,1)S(1)}, u32[]{:S(2)}, u32[]{:S(2)}) collective-permute-start(bf16[2,256,256]{1,2,0:T(8,128)(2,1)S(1)} %pad_maximum_fusion), channel_id=1, source_target_pairs={{0,128},{64,192},{128,0},{192,64},{256,384},{320,448},{384,256},{4... | collective-permute-start | bytes 786440 | tf_op jit(solution)/shard_map/ppermute | solution.py:18
  114.6 29.5 %collective-permute-start.2 = (bf16[2,256,256]{1,2,0:T(8,128)(2,1)S(1)}, bf16[2,256,256]{1,2,0:T(8,128)(2,1)S(1)}, u32[]{:S(2)}, u32[]{:S(2)}) collective-permute-start(bf16[2,256,256]{1,2,0:T(8,128)(2,1)S(1)} %pad_maximum_fusion.1), channel_id=1, source_target_pairs={{0,256},{64,320},{128,384},{192,448},{256,0},{320,64},{384,128},{4... | collective-permute-start | bytes 786440 | tf_op jit(solution)/shard_map/ppermute | solution.py:18
where the time goes:
time: 149 us; the launch traced here: 148 us
  waiting for transfers between devices  63.9 us (43%)
  starting transfers between devices  47.4 us (32%)
  local copies, waits for them, and re-layouts  20.5 us (14%)
  other arithmetic  11 us (7%)
  matrix products  4.97 us (3%)
    ppermute x3, waiting for transfers between devices, partner(): lax.ppermute(array, axis, [(i, i ^ 1 << apart) for i in range(lax.axis_si...  45.3 us
    ppermute x3, starting transfers between devices, partner(): lax.ppermute(array, axis, [(i, i ^ 1 << apart) for i in range(lax.axis_si...  25.2 us
    all_to_all x1, starting transfers between devices, per_device(): lax.all_to_all(layout, 'gate', split_axis=2, concat_axis=1, tiled=True)  22.2 us
    all_to_all x1, waiting for transfers between devices, per_device(): lax.all_to_all(layout, 'gate', split_axis=2, concat_axis=1, tiled=True)  18.5 us
    gather x24, local copies, waits for them, and re-layouts  16.7 us
    another operation x7, other arithmetic  10.4 us
  transfers between devices with their start and end apart: 4, of which 4 were waited for; matrix products, arithmetic and copies ran while one was open for 2% of the time, Pallas kernels for 0%

commit v1 on v0

v1 whole, which is shorter than its diff:
```python
import functools
import math

import jax
import jax.numpy as jnp
import ml_dtypes
import numpy as np
from jax import lax
from jax.experimental import pallas as pl
from jax.experimental.pallas import tpu as pltpu
from jax.sharding import PartitionSpec as P

RADIX = 128
SAMPLES = 16384
ANGLES = 256
SUB_PULSES = 512
N_SUB = 8
HALVES = 2
PEERS = 32
RING = HALVES * N_SUB
OWN = 8
BLOCK = 256
WINDOW = 44
ROWS = 2 * WINDOW
STARTS = (0, 26, 60, 84)
TWO_PI = 2.0 * math.pi
MESH = pl.DeviceIdType.MESH


def bf16(values):
    return values.astype(ml_dtypes.bfloat16)


def complex_rows(table):
    return np.block([[table.real, -table.imag], [table.imag, table.real]])


def dft_matrix():
    count = np.arange(RADIX)
    turns = (count[:, None] * count[None, :]) % RADIX
    return bf16(complex_rows(np.exp(-1j * TWO_PI / RADIX * turns) / math.sqrt(RADIX)))


def twiddle_table():
    count = np.arange(RADIX)
    turns = np.exp(-1j * TWO_PI / SAMPLES * (count[:, None] * count[None, :]))
    return np.stack([turns.real, turns.imag]).astype(np.float32)


def steer_matrix():
    beams = np.concatenate(
        [128 * (q // 4) + STARTS[q % 4] + np.arange(WINDOW) for q in range(N_SUB)]
    )
    halves = []
    for half in range(HALVES):
        pulses = half * PEERS * OWN + np.arange(PEERS * OWN)
        turns = ((2 * beams[:, None] - ANGLES + 1) * (2 * pulses[None, :] - SUB_PULSES + 1)) % 4096
        table = np.exp(-1j * TWO_PI / 4096 * turns) / math.sqrt(SUB_PULSES)
        table = table.reshape(N_SUB, WINDOW, PEERS, OWN)
        upper = np.stack([table.real, -table.imag], axis=3)
        lower = np.stack([table.imag, table.real], axis=3)
        halves.append(np.stack([upper, lower], axis=1).reshape(N_SUB * ROWS, PEERS * 2 * OWN))
    return bf16(np.stack(halves))


def interp_matrix():
    distance = np.arange(ANGLES)[:, None] / 2 - 0.25 - np.arange(ANGLES // 2)[None, :]
    taper = np.where(np.abs(distance) < 4.0, 0.5 + 0.5 * np.cos(math.pi * distance / 4.0), 0.0)
    return bf16(np.sinc(distance) * taper).astype(np.float64)


def turned(rows, member):
    sign = 1 - 2 * member
    return np.exp(sign * 1j * TWO_PI * (2 * rows + 1) / 16)[:, None] / math.sqrt(2.0)


def merge_matrices():
    interp = interp_matrix()
    rows = np.arange(ANGLES)
    half = ANGLES // 2
    early = []
    for kind in range(4):
        second = slice(half * (kind % 2), half * (kind % 2) + half)
        first = slice(half * (kind // 2), half * (kind // 2) + half)
        blocks = []
        for late in range(2):
            for soon in range(2):
                two = (turned(rows, late) * interp)[second]
                one = (turned(rows, soon) * interp)[first]
                window = (two @ one)[:, STARTS[kind] : STARTS[kind] + WINDOW]
                blocks.append(complex_rows(window))
        early.append(np.concatenate(blocks, axis=1))
    last = [complex_rows(turned(rows, member) * interp) for member in range(2)]
    return bf16(np.stack(early)), bf16(np.concatenate(last, axis=1))


def swapped_bits(value):
    return value % 2 * 4 + value // 2 % 2 * 2 + value // 4


def kernel(
    delays,
    raw,
    dft,
    twiddle,
    last,
    steer_all,
    early_all,
    image,
    steer,
    early,
    spread,
    packed,
    twisted,
    rolled,
    blocks,
    pulses,
    outgoing,
    incoming,
    table_sem,
    plane_send,
    plane_recv,
    ring_send,
    ring_recv,
):
    sub = lax.axis_index("sub")
    gate = lax.axis_index("gate")
    half = gate // PEERS
    peer = gate % PEERS
    place = half * N_SUB + sub
    sector = swapped_bits(sub)

    barrier = pltpu.get_barrier_semaphore()

    def greet_plane(step, carry):
        other = half * PEERS + (peer + step) % PEERS
        pl.semaphore_signal(barrier, inc=1, device_id={"gate": other}, device_id_type=MESH)
        return carry

    def greet_ring(step, carry):
        spot = (place + step) % RING
        to = {"sub": spot % N_SUB, "gate": spot // N_SUB * PEERS + peer}
        pl.semaphore_signal(barrier, inc=1, device_id=to, device_id_type=MESH)
        return carry

    lax.fori_loop(1, RING, greet_ring, 0)
    lax.fori_loop(1, PEERS, greet_plane, 0)

    load_steer = pltpu.make_async_copy(steer_all.at[half], steer, table_sem.at[0])
    load_steer.start()
    load_early = pltpu.make_async_copy(early_all.at[sector % 4], early, table_sem.at[1])
    load_early.start()

    for part in range(2):
        spread[part] = raw[part].astype(jnp.float32).reshape(RADIX * OWN, RADIX)
    for part in range(2):
        for pulse in range(OWN):
            packed[part * RADIX : (part + 1) * RADIX, pulse * RADIX : (pulse + 1) * RADIX] = spread[
                part, pl.ds(pulse, RADIX, stride=OWN), :
            ].astype(jnp.bfloat16)
    cosine = twiddle[0]
    sine = twiddle[1]
    for pair in range(OWN // 2):
        section = jnp.dot(
            dft[...],
            packed[:, pair * 2 * RADIX : (pair + 1) * 2 * RADIX],
            preferred_element_type=jnp.float32,
        )
        for side in range(2):
            real = section[:RADIX, side * RADIX : (side + 1) * RADIX]
            imag = section[RADIX:, side * RADIX : (side + 1) * RADIX]
            rows = slice((2 * pair + side) * RADIX, (2 * pair + side + 1) * RADIX)
            twisted[rows, :RADIX] = (real * cosine - imag * sine).astype(jnp.bfloat16)
            twisted[rows, RADIX:] = (real * sine + imag * cosine).astype(jnp.bfloat16)
    lane = lax.broadcasted_iota(jnp.int32, (RADIX, RADIX), 1)
    for part in range(2):
        rolled[part, RADIX:, :] = jnp.zeros((8, RADIX), jnp.float32)
    for pair in range(OWN // 2):
        spectrum = lax.dot_general(
            dft[...],
            twisted[pair * 2 * RADIX : (pair + 1) * 2 * RADIX, :],
            (((1,), (1,)), ((), ())),
            preferred_element_type=jnp.float32,
        )
        for side in range(2):
            pulse = 2 * pair + side
            delay = delays[pulse]
            near = lane < RADIX - delay
            for part in range(2):
                own = spectrum[part * RADIX : (part + 1) * RADIX, side * RADIX : (side + 1) * RADIX]
                own = pltpu.roll(own, RADIX - delay, 1)
                rolled[part, :RADIX, :] = own
                after = rolled[part, 1 : RADIX + 1, :]
                spread[part, pl.ds(pulse, RADIX, stride=OWN), :] = jnp.where(near, own, after)
    rows = jnp.concatenate(
        [spread[part].reshape(RADIX, OWN, RADIX) for part in range(2)], axis=1
    ).astype(jnp.bfloat16)
    rows = rows.reshape(HALVES * PEERS, 2, 2 * OWN, RADIX)
    for side in range(2):
        blocks[:, :, :, side * RADIX : (side + 1) * RADIX] = rows[:, side].reshape(
            HALVES, PEERS, 2 * OWN, RADIX
        )

    pl.semaphore_wait(barrier, RING - 1 + PEERS - 1)

    def plane_copy(step):
        other = (peer + step) % PEERS
        return pltpu.make_async_remote_copy(
            src_ref=blocks.at[:, other],
            dst_ref=pulses.at[:, peer],
            send_sem=plane_send.at[step],
            recv_sem=plane_recv.at[step],
            device_id={"gate": half * PEERS + other},
            device_id_type=MESH,
        )

    def plane_start(step, carry):
        plane_copy(step).start()
        return carry

    lax.fori_loop(1, PEERS, plane_start, 0)
    for side in range(HALVES):
        pulses[side, peer] = blocks[side, peer]
    load_steer.wait()
    load_early.wait()

    def plane_wait(step, carry):
        plane_copy(step).wait()
        return carry

    lax.fori_loop(1, PEERS, plane_wait, 0)

    for side in range(HALVES):
        beams = jnp.dot(
            steer[...],
            pulses[side].reshape(PEERS * 2 * OWN, BLOCK),
            preferred_element_type=jnp.float32,
        )
        for q in range(N_SUB):
            window = beams[q * ROWS : (q + 1) * ROWS]
            outgoing[side, q] = jnp.concatenate(
                [window[:, :RADIX], window[:, RADIX:]], axis=0
            ).astype(jnp.bfloat16)

    def ring_copy(step):
        spot = (place + step) % RING
        there = spot % N_SUB
        return pltpu.make_async_remote_copy(
            src_ref=outgoing.at[spot // N_SUB, swapped_bits(there)],
            dst_ref=incoming.at[half, sub],
            send_sem=ring_send.at[step],
            recv_sem=ring_recv.at[step],
            device_id={"sub": there, "gate": spot // N_SUB * PEERS + peer},
            device_id_type=MESH,
        )

    for distance in range(RING // 2, 0, -1):
        ring_copy(distance).start()
        if distance < RING // 2:
            ring_copy(RING - distance).start()
    incoming[half, sub] = outgoing[half, sector]

    position = (
        gate * BLOCK + lax.broadcasted_iota(jnp.int32, (1, BLOCK), 1) + SAMPLES
    ).astype(jnp.float32)
    phase = (-TWO_PI * 84.0) / position
    gate_cos = jnp.cos(phase)
    gate_sin = jnp.sin(phase)

    def ring_wait(step, carry):
        ring_copy(step).wait()
        return carry

    lax.fori_loop(1, RING, ring_wait, 0)

    total = None
    for late in range(2):
        children = []
        for s in range(4 * late, 4 * late + 4):
            both = incoming[0, s].astype(jnp.float32) + incoming[1, s].astype(jnp.float32)
            children.append(
                jnp.concatenate([both[:ROWS], both[ROWS:]], axis=1).astype(jnp.bfloat16)
            )
        level_two = jnp.dot(
            early[...], jnp.concatenate(children, axis=0), preferred_element_type=jnp.float32
        ).astype(jnp.bfloat16)
        made = jnp.dot(
            last[:, late * ANGLES : (late + 1) * ANGLES],
            level_two,
            preferred_element_type=jnp.float32,
        )
        total = made if total is None else total + made
    real = total[:ANGLES]
    imag = total[ANGLES:]
    image[0] = (real * gate_cos - imag * gate_sin).astype(jnp.bfloat16)
    image[1] = (real * gate_sin + imag * gate_cos).astype(jnp.bfloat16)


def per_device(raw_echo, delays):
    raw = raw_echo.reshape(2, OWN, RADIX, RADIX).transpose(0, 2, 1, 3)
    early, last = merge_matrices()
    vmem = pl.BlockSpec(memory_space=pltpu.VMEM)
    hbm = pl.BlockSpec(memory_space=pl.ANY)
    return pl.pallas_call(
        kernel,
        out_shape=jax.ShapeDtypeStruct((2, ANGLES, BLOCK), jnp.bfloat16),
        in_specs=[pl.BlockSpec(memory_space=pltpu.SMEM), vmem, vmem, vmem, vmem, hbm, hbm],
        out_specs=vmem,
        scratch_shapes=[
            pltpu.VMEM((N_SUB * ROWS, PEERS * 2 * OWN), jnp.bfloat16),
            pltpu.VMEM((ANGLES, 4 * ROWS), jnp.bfloat16),
            pltpu.VMEM((2, RADIX * OWN, RADIX), jnp.float32),
            pltpu.VMEM((2 * RADIX, OWN * RADIX), jnp.bfloat16),
            pltpu.VMEM((OWN * RADIX, 2 * RADIX), jnp.bfloat16),
            pltpu.VMEM((2, RADIX + 8, RADIX), jnp.float32),
            pltpu.VMEM((HALVES, PEERS, 2 * OWN, BLOCK), jnp.bfloat16),
            pltpu.VMEM((HALVES, PEERS, 2 * OWN, BLOCK), jnp.bfloat16),
            pltpu.VMEM((HALVES, N_SUB, 2 * ROWS, RADIX), jnp.bfloat16),
            pltpu.VMEM((HALVES, N_SUB, 2 * ROWS, RADIX), jnp.bfloat16),
            pltpu.SemaphoreType.DMA((2,)),
            pltpu.SemaphoreType.DMA((PEERS,)),
            pltpu.SemaphoreType.DMA((PEERS,)),
            pltpu.SemaphoreType.DMA((RING,)),
            pltpu.SemaphoreType.DMA((RING,)),
        ],
        compiler_params=pltpu.CompilerParams(collective_id=0, has_side_effects=True),
        name="image_formation",
    )(
        delays,
        raw,
        jnp.asarray(dft_matrix()),
        jnp.asarray(twiddle_table()),
        jnp.asarray(last),
        jnp.asarray(steer_matrix()),
        jnp.asarray(early),
    )


def solution(mesh):
    placed = (P(None, ("sub", "gate"), None), P(("sub", "gate")))
    return jax.shard_map(
        per_device, mesh=mesh, in_specs=placed, out_specs=P(None, "sub", "gate"), check_vma=False
    )
```

time: 149 us -> 65.2 us (0.44)
  waiting for transfers between devices: 63.9 us -> 0 us
  Pallas kernels: 0 us -> 63.3 us
  starting transfers between devices: 47.4 us -> 0 us
  local copies, waits for them, and re-layouts: 20.5 us -> 1.67 us
  other arithmetic: 11 us -> 0 us
  matrix products: 4.97 us -> 0 us
    pallas_call x0 -> x1, Pallas kernels: none -> 63.3 us  [per_device(): pl.pallas_call(kernel, out_shape=jax.ShapeDtypeStruct((2, ANGLES, BLOCK),...]
    ppermute x3 -> x0, waiting for transfers between devices: 45.3 us -> none  [partner(): lax.ppermute(array, axis, [(i, i ^ 1 << apart) for i in range(lax.axis_si...]
    ppermute x3 -> x0, starting transfers between devices: 25.2 us -> none  [partner(): lax.ppermute(array, axis, [(i, i ^ 1 << apart) for i in range(lax.axis_si...]
    all_to_all x1 -> x0, starting transfers between devices: 22.2 us -> none  [per_device(): lax.all_to_all(layout, 'gate', split_axis=2, concat_axis=1, tiled=True)]
    all_to_all x1 -> x0, waiting for transfers between devices: 18.5 us -> none  [per_device(): lax.all_to_all(layout, 'gate', split_axis=2, concat_axis=1, tiled=True)]
    gather x24 -> x0, local copies, waits for them, and re-layouts: 16.7 us -> none
    another operation x14 -> x0, other arithmetic: 10.6 us -> none
    dot_general x6 -> x0, matrix products: 4.97 us -> none  [the longest x3 2.86 us: merge_pair(): jnp.einsum('jh,kchg->kcjg', interp_table(ANGLES), paired, preferred_eleme...]
  transfers between devices with their start and end apart: 4 -> 0, of which waited for: 4 -> 0; matrix products, arithmetic and copies ran while one was open for 2% -> 0% of each run, Pallas kernels for 0% -> 0%
where the time goes in v1:
time: 65.2 us; the launch traced here: 65 us
  Pallas kernels  63.3 us (97%)
  local copies, waits for them, and re-layouts  1.67 us (3%)
    pallas_call x1, Pallas kernels, per_device(): pl.pallas_call(kernel, out_shape=jax.ShapeDtypeStruct((2, ANGLES, BLOCK),...  63.3 us
    unnamed x1, local copies, waits for them, and re-layouts  1.67 us

profile of v1, /device:TPU:1, one launch (start us, length us, event | category | flops | bytes accessed | tf_op | source)
XLA Modules:
  0.0 65.0 jit_solution(6743076773439765025)
XLA Ops:
  0.0 63.3 %image_formation.1 = bf16[2,256,256]{2,1,0:T(8,128)(2,1)} custom-call(s32[8]{0:T(128)} %delays.1, bf16[2,128,8,128]{3,2,1,0:T(8,128)(2,1)} %bitcast.3, bf16[256,256]{1,0:T(8,128)(2,1)} %constant.10.clone.dft, f32[2,128,128]{2,1,0:T(8,128)} %constant.11.clone.twiddle, bf16[512,512]{1,0:T(8,128)(2,1)} %constant.12.clone.last, ...), custom_call_target="tpu_custom_call" | custom-call | tf_op jit(solution)/shard_map/image_formation/pallas_call | solution.py:304
  63.3 1.7 %copy.9 = bf16[2,256,256]{2,1,0:T(8,128)(2,1)} copy(bf16[2,256,256]{2,1,0:T(8,128)(2,1)} %image_formation.1) | data formatting | bytes 524288

commit v2 on v1

--- a/solution.py
+++ b/solution.py
@@ -22,6 +22,7 @@
 BLOCK = 256
 WINDOW = 44
 ROWS = 2 * WINDOW
+HELD = RADIX // HALVES + 8
 STARTS = (0, 26, 60, 84)
 TWO_PI = 2.0 * math.pi
 MESH = pl.DeviceIdType.MESH
@@ -35,10 +36,18 @@
     return np.block([[table.real, -table.imag], [table.imag, table.real]])
 
 
-def dft_matrix():
+def dft_matrices():
     count = np.arange(RADIX)
     turns = (count[:, None] * count[None, :]) % RADIX
-    return bf16(complex_rows(np.exp(-1j * TWO_PI / RADIX * turns) / math.sqrt(RADIX)))
+    table = np.exp(-1j * TWO_PI / RADIX * turns) / math.sqrt(RADIX)
+    part = RADIX // HALVES
+    rows = np.concatenate([table, np.zeros((8, RADIX))])
+    halves = []
+    for half in range(HALVES):
+        own = rows[half * part : half * part + HELD].copy()
+        own[part + 1 :] = 0
+        halves.append(complex_rows(own))
+    return bf16(complex_rows(table)), bf16(np.stack(halves))
 
 
 def twiddle_table():
@@ -102,6 +111,7 @@
     delays,
     raw,
     dft,
+    dft_half,
     twiddle,
     last,
     steer_all,
@@ -117,6 +127,7 @@
     pulses,
     outgoing,
     incoming,
+    ready,
     table_sem,
     plane_send,
     plane_recv,
@@ -132,6 +143,9 @@
 
     barrier = pltpu.get_barrier_semaphore()
 
+    def at(spot):
+        return {"sub": spot % N_SUB, "gate": spot // N_SUB * PEERS + peer}
+
     def greet_plane(step, carry):
         other = half * PEERS + (peer + step) % PEERS
         pl.semaphore_signal(barrier, inc=1, device_id={"gate": other}, device_id_type=MESH)
@@ -139,12 +153,26 @@
 
     def greet_ring(step, carry):
         spot = (place + step) % RING
-        to = {"sub": spot % N_SUB, "gate": spot // N_SUB * PEERS + peer}
-        pl.semaphore_signal(barrier, inc=1, device_id=to, device_id_type=MESH)
+
+        @pl.when(spot > place)
+        def _():
+            pl.semaphore_signal(barrier, inc=1, device_id=at(spot), device_id_type=MESH)
+
         return carry
 
+    def answer_ring(step, carry):
+        spot = (place + step) % RING
+
+        @pl.when(spot < place)
+        def _():
+            pl.semaphore_signal(
+                ready.at[place], inc=1, device_id=at(spot), device_id_type=MESH
+            )
+
+        return carry
+
+    lax.fori_loop(1, PEERS, greet_plane, 0)
     lax.fori_loop(1, RING, greet_ring, 0)
-    lax.fori_loop(1, PEERS, greet_plane, 0)
 
     load_steer = pltpu.make_async_copy(steer_all.at[half], steer, table_sem.at[0])
     load_steer.start()
@@ -172,65 +200,68 @@
             rows = slice((2 * pair + side) * RADIX, (2 * pair + side + 1) * RADIX)
             twisted[rows, :RADIX] = (real * cosine - imag * sine).astype(jnp.bfloat16)
             twisted[rows, RADIX:] = (real * sine + imag * cosine).astype(jnp.bfloat16)
-    lane = lax.broadcasted_iota(jnp.int32, (RADIX, RADIX), 1)
-    for part in range(2):
-        rolled[part, RADIX:, :] = jnp.zeros((8, RADIX), jnp.float32)
-    for pair in range(OWN // 2):
-        spectrum = lax.dot_general(
-            dft[...],
-            twisted[pair * 2 * RADIX : (pair + 1) * 2 * RADIX, :],
-            (((1,), (1,)), ((), ())),
-            preferred_element_type=jnp.float32,
-        )
-        for side in range(2):
-            pulse = 2 * pair + side
-            delay = delays[pulse]
-            near = lane < RADIX - delay
-            for part in range(2):
-                own = spectrum[part * RADIX : (part + 1) * RADIX, side * RADIX : (side + 1) * RADIX]
-                own = pltpu.roll(own, RADIX - delay, 1)
-                rolled[part, :RADIX, :] = own
-                after = rolled[part, 1 : RADIX + 1, :]
-                spread[part, pl.ds(pulse, RADIX, stride=OWN), :] = jnp.where(near, own, after)
-    rows = jnp.concatenate(
-        [spread[part].reshape(RADIX, OWN, RADIX) for part in range(2)], axis=1
-    ).astype(jnp.bfloat16)
-    rows = rows.reshape(HALVES * PEERS, 2, 2 * OWN, RADIX)
-    for side in range(2):
-        blocks[:, :, :, side * RADIX : (side + 1) * RADIX] = rows[:, side].reshape(
-            HALVES, PEERS, 2 * OWN, RADIX
-        )
-
-    pl.semaphore_wait(barrier, RING - 1 + PEERS - 1)
-
-    def plane_copy(step):
+    lane = lax.broadcasted_iota(jnp.int32, (RADIX // HALVES, RADIX), 1)
+
+    def range_gates(side):
+        count = RADIX // HALVES
+        for pair in range(OWN // 2):
+            spectrum = lax.dot_general(
+                dft_half[side],
+                twisted[pair * 2 * RADIX : (pair + 1) * 2 * RADIX, :],
+                (((1,), (1,)), ((), ())),
+                preferred_element_type=jnp.float32,
+            )
+            for late in range(2):
+                pulse = 2 * pair + late
+                delay = delays[pulse]
+                near = lane < RADIX - delay
+                for part in range(2):
+                    own = pltpu.roll(
+                        spectrum[
+                            part * HELD : (part + 1) * HELD, late * RADIX : (late + 1) * RADIX
+                        ],
+                        RADIX - delay,
+                        1,
+                    )
+                    rolled[part, :, :] = own
+                    after = rolled[part, 1 : count + 1, :]
+                    spread[part, pl.ds(pulse, count, stride=OWN), :] = jnp.where(
+                        near, own[:count], after
+                    )
+        rows = jnp.concatenate(
+            [spread[part, : count * OWN].reshape(count, OWN, RADIX) for part in range(2)], axis=1
+        ).astype(jnp.bfloat16)
+        rows = rows.reshape(PEERS, 2, 2 * OWN, RADIX)
+        for late in range(2):
+            blocks[side, :, :, late * RADIX : (late + 1) * RADIX] = rows[:, late]
+
+    def plane_copy(side, step):
         other = (peer + step) % PEERS
         return pltpu.make_async_remote_copy(
-            src_ref=blocks.at[:, other],
-            dst_ref=pulses.at[:, peer],
-            send_sem=plane_send.at[step],
-            recv_sem=plane_recv.at[step],
+            src_ref=blocks.at[side, other],
+            dst_ref=pulses.at[side, peer],
+            send_sem=plane_send.at[side, step],
+            recv_sem=plane_recv.at[side, step],
             device_id={"gate": half * PEERS + other},
             device_id_type=MESH,
         )
 
-    def plane_start(step, carry):
-        plane_copy(step).start()
-        return carry
-
-    lax.fori_loop(1, PEERS, plane_start, 0)
-    for side in range(HALVES):
+    def plane_starts(side):
+        def start(step, carry):
+            plane_copy(side, step).start()
+            return carry
+
+        lax.fori_loop(1, PEERS, start, 0)
         pulses[side, peer] = blocks[side, peer]
-    load_steer.wait()
-    load_early.wait()
-
-    def plane_wait(step, carry):
-        plane_copy(step).wait()
-        return carry
-
-    lax.fori_loop(1, PEERS, plane_wait, 0)
-
-    for side in range(HALVES):
+
+    def plane_waits(side):
+        def wait(step, carry):
+            plane_copy(side, step).wait()
+            return carry
+
+        lax.fori_loop(1, PEERS, wait, 0)
+
+    def beam_sums(side):
         beams = jnp.dot(
             steer[...],
             pulses[side].reshape(PEERS * 2 * OWN, BLOCK),
@@ -244,20 +275,45 @@
 
     def ring_copy(step):
         spot = (place + step) % RING
-        there = spot % N_SUB
         return pltpu.make_async_remote_copy(
-            src_ref=outgoing.at[spot // N_SUB, swapped_bits(there)],
+            src_ref=outgoing.at[spot // N_SUB, swapped_bits(spot % N_SUB)],
             dst_ref=incoming.at[half, sub],
             send_sem=ring_send.at[step],
             recv_sem=ring_recv.at[step],
-            device_id={"sub": there, "gate": spot // N_SUB * PEERS + peer},
+            device_id=at(spot),
             device_id_type=MESH,
         )
 
-    for distance in range(RING // 2, 0, -1):
-        ring_copy(distance).start()
-        if distance < RING // 2:
-            ring_copy(RING - distance).start()
+    def ring_starts(side):
+        def start(turn, carry):
+            distance = RING // 2 - (turn + 1) // 2
+            step = jnp.where(turn % 2 == 0, RING - distance, distance)
+            spot = (place + step) % RING
+
+            @pl.when(spot // N_SUB == side)
+            def _():
+                @pl.when(spot > place)
+                def _():
+                    pl.semaphore_wait(ready.at[spot], 1)
+
+                ring_copy(step).start()
+
+            return carry
+
+        lax.fori_loop(0, RING - 1, start, 0)
+
+    range_gates(0)
+    pl.semaphore_wait(barrier, PEERS - 1 + place)
+    plane_starts(0)
+    lax.fori_loop(1, RING, answer_ring, 0)
+    range_gates(1)
+    plane_starts(1)
+    load_steer.wait()
+    load_early.wait()
+    for side in range(HALVES):
+        plane_waits(side)
+        beam_sums(side)
+        ring_starts(side)
     incoming[half, sub] = outgoing[half, sector]
 
     position = (
@@ -299,12 +355,13 @@
 def per_device(raw_echo, delays):
     raw = raw_echo.reshape(2, OWN, RADIX, RADIX).transpose(0, 2, 1, 3)
     early, last = merge_matrices()
+    dft, dft_half = dft_matrices()
     vmem = pl.BlockSpec(memory_space=pltpu.VMEM)
     hbm = pl.BlockSpec(memory_space=pl.ANY)
     return pl.pallas_call(
         kernel,
         out_shape=jax.ShapeDtypeStruct((2, ANGLES, BLOCK), jnp.bfloat16),
-        in_specs=[pl.BlockSpec(memory_space=pltpu.SMEM), vmem, vmem, vmem, vmem, hbm, hbm],
+        in_specs=[pl.BlockSpec(memory_space=pltpu.SMEM), vmem, vmem, vmem, vmem, vmem, hbm, hbm],
         out_specs=vmem,
         scratch_shapes=[
             pltpu.VMEM((N_SUB * ROWS, PEERS * 2 * OWN), jnp.bfloat16),
@@ -312,14 +369,15 @@
             pltpu.VMEM((2, RADIX * OWN, RADIX), jnp.float32),
             pltpu.VMEM((2 * RADIX, OWN * RADIX), jnp.bfloat16),
             pltpu.VMEM((OWN * RADIX, 2 * RADIX), jnp.bfloat16),
-            pltpu.VMEM((2, RADIX + 8, RADIX), jnp.float32),
+            pltpu.VMEM((2, HELD, RADIX), jnp.float32),
             pltpu.VMEM((HALVES, PEERS, 2 * OWN, BLOCK), jnp.bfloat16),
             pltpu.VMEM((HALVES, PEERS, 2 * OWN, BLOCK), jnp.bfloat16),
             pltpu.VMEM((HALVES, N_SUB, 2 * ROWS, RADIX), jnp.bfloat16),
             pltpu.VMEM((HALVES, N_SUB, 2 * ROWS, RADIX), jnp.bfloat16),
+            pltpu.SemaphoreType.REGULAR((RING,)),
             pltpu.SemaphoreType.DMA((2,)),
-            pltpu.SemaphoreType.DMA((PEERS,)),
-            pltpu.SemaphoreType.DMA((PEERS,)),
+            pltpu.SemaphoreType.DMA((HALVES, PEERS)),
+            pltpu.SemaphoreType.DMA((HALVES, PEERS)),
             pltpu.SemaphoreType.DMA((RING,)),
             pltpu.SemaphoreType.DMA((RING,)),
         ],
@@ -328,7 +386,8 @@
     )(
         delays,
         raw,
-        jnp.asarray(dft_matrix()),
+        jnp.asarray(dft),
+        jnp.asarray(dft_half),
         jnp.asarray(twiddle_table()),
         jnp.asarray(last),
         jnp.asarray(steer_matrix()),

time: 65.2 us -> 64.4 us (0.988)
  Pallas kernels: 63.3 us -> 62.5 us
    pallas_call x1, Pallas kernels: 63.3 us -> 62.5 us  [per_device(): pl.pallas_call(kernel, out_shape=jax.ShapeDtypeStruct((2, ANGLES, BLOCK),...]
where the time goes in v2:
time: 64.4 us; the launch traced here: 64.2 us
  Pallas kernels  62.5 us (97%)
  local copies, waits for them, and re-layouts  1.67 us (3%)
    pallas_call x1, Pallas kernels, per_device(): pl.pallas_call(kernel, out_shape=jax.ShapeDtypeStruct((2, ANGLES, BLOCK),...  62.5 us
    unnamed x1, local copies, waits for them, and re-layouts  1.67 us

profile of v2, /device:TPU:1, one launch (start us, length us, event | category | flops | bytes accessed | tf_op | source)
XLA Modules:
  0.0 64.2 jit_solution(110325938345957368)
XLA Ops:
  0.0 62.5 %image_formation.1 = bf16[2,256,256]{2,1,0:T(8,128)(2,1)} custom-call(s32[8]{0:T(128)} %delays.1, bf16[2,128,8,128]{3,2,1,0:T(8,128)(2,1)} %bitcast.3, bf16[256,256]{1,0:T(8,128)(2,1)} %constant.12.clone.dft, bf16[2,144,256]{2,1,0:T(8,128)(2,1)} %constant.13.clone.dft_half, f32[2,128,128]{2,1,0:T(8,128)} %constant.14.clone.twiddle, ...), custom_call_target="tpu_custom_call" | custom-call | tf_op jit(solution)/shard_map/image_formation/pallas_call | solution.py:361
  62.5 1.7 %copy.10 = bf16[2,256,256]{2,1,0:T(8,128)(2,1)} copy(bf16[2,256,256]{2,1,0:T(8,128)(2,1)} %image_formation.1) | data formatting | bytes 524288

commit v3 on v2

--- a/solution.py
+++ b/solution.py
@@ -20,10 +20,15 @@
 RING = HALVES * N_SUB
 OWN = 8
 BLOCK = 256
-WINDOW = 44
-ROWS = 2 * WINDOW
+WINDOW = 42
+EDGE_WINDOW = 38
+ROWS = 88
+TILES = 21
+EDGE_TILES = 19
+ALL_TILES = N_SUB * (TILES + EDGE_TILES)
 HELD = RADIX // HALVES + 8
-STARTS = (0, 26, 60, 84)
+STARTS = (0, 26, 60, 90)
+WIDTHS = (EDGE_WINDOW, WINDOW, WINDOW, EDGE_WINDOW)
 TWO_PI = 2.0 * math.pi
 MESH = pl.DeviceIdType.MESH
 
@@ -57,19 +62,19 @@
 
 
 def steer_matrix():
-    beams = np.concatenate(
-        [128 * (q // 4) + STARTS[q % 4] + np.arange(WINDOW) for q in range(N_SUB)]
-    )
-    halves = []
+    result = np.zeros((HALVES, N_SUB, ROWS, PEERS * 2 * OWN))
     for half in range(HALVES):
         pulses = half * PEERS * OWN + np.arange(PEERS * OWN)
-        turns = ((2 * beams[:, None] - ANGLES + 1) * (2 * pulses[None, :] - SUB_PULSES + 1)) % 4096
-        table = np.exp(-1j * TWO_PI / 4096 * turns) / math.sqrt(SUB_PULSES)
-        table = table.reshape(N_SUB, WINDOW, PEERS, OWN)
-        upper = np.stack([table.real, -table.imag], axis=3)
-        lower = np.stack([table.imag, table.real], axis=3)
-        halves.append(np.stack([upper, lower], axis=1).reshape(N_SUB * ROWS, PEERS * 2 * OWN))
-    return bf16(np.stack(halves))
+        for q in range(N_SUB):
+            beams = 128 * (q // 4) + STARTS[q % 4] + np.arange(WIDTHS[q % 4])
+            turns = (2 * beams[:, None] - ANGLES + 1) * (2 * pulses[None, :] - SUB_PULSES + 1)
+            table = np.exp(-1j * TWO_PI / 4096 * (turns % 4096)) / math.sqrt(SUB_PULSES)
+            table = table.reshape(-1, PEERS, OWN)
+            upper = np.stack([table.real, -table.imag], axis=2)
+            lower = np.stack([table.imag, table.real], axis=2)
+            rows = np.stack([upper, lower], axis=1).reshape(-1, PEERS * 2 * OWN)
+            result[half, q, : len(rows)] = rows
+    return bf16(result.reshape(HALVES, N_SUB * ROWS, PEERS * 2 * OWN))
 
 
 def interp_matrix():
@@ -96,27 +101,39 @@
             for soon in range(2):
                 two = (turned(rows, late) * interp)[second]
                 one = (turned(rows, soon) * interp)[first]
-                window = (two @ one)[:, STARTS[kind] : STARTS[kind] + WINDOW]
-                blocks.append(complex_rows(window))
+                window = (two @ one)[:, STARTS[kind] : STARTS[kind] + WIDTHS[kind]]
+                columns = complex_rows(window).reshape(2 * half, 2, -1).transpose(0, 2, 1)
+                columns = columns.reshape(2 * half, -1)
+                blocks.append(np.pad(columns, ((0, 0), (0, ROWS - columns.shape[1]))))
         early.append(np.concatenate(blocks, axis=1))
     last = [complex_rows(turned(rows, member) * interp) for member in range(2)]
     return bf16(np.stack(early)), bf16(np.concatenate(last, axis=1))
 
 
+def bits(value):
+    return lax.rem(value, 2), lax.rem(lax.div(value, 2), 2), lax.div(value, 4)
+
+
 def swapped_bits(value):
-    return value % 2 * 4 + value // 2 % 2 * 2 + value // 4
+    low, middle, high = bits(value)
+    return low * 4 + middle * 2 + high
 
 
 def kernel(
     delays,
+    raw_in,
+    dft_in,
+    dft_half_in,
+    twiddle_in,
+    last_in,
+    steer_in,
+    early_in,
+    image,
     raw,
     dft,
     dft_half,
     twiddle,
     last,
-    steer_all,
-    early_all,
-    image,
     steer,
     early,
     spread,
@@ -136,48 +153,51 @@
 ):
     sub = lax.axis_index("sub")
     gate = lax.axis_index("gate")
-    half = gate // PEERS
-    peer = gate % PEERS
+    half = lax.div(gate, PEERS)
+    peer = lax.rem(gate, PEERS)
     place = half * N_SUB + sub
     sector = swapped_bits(sub)
 
+    loads = [
+        pltpu.make_async_copy(source, target, table_sem.at[i])
+        for i, (source, target) in enumerate(
+            (
+                (raw_in, raw),
+                (dft_in, dft),
+                (twiddle_in, twiddle),
+                (dft_half_in, dft_half),
+                (steer_in.at[half], steer),
+                (early_in.at[lax.rem(sector, 4)], early),
+                (last_in, last),
+            )
+        )
+    ]
+    for load in loads:
+        load.start()
+
     barrier = pltpu.get_barrier_semaphore()
 
     def at(spot):
-        return {"sub": spot % N_SUB, "gate": spot // N_SUB * PEERS + peer}
+        return {"sub": lax.rem(spot, N_SUB), "gate": lax.div(spot, N_SUB) * PEERS + peer}
 
     def greet_plane(step, carry):
-        other = half * PEERS + (peer + step) % PEERS
+        other = half * PEERS + lax.rem(peer + step, PEERS)
         pl.semaphore_signal(barrier, inc=1, device_id={"gate": other}, device_id_type=MESH)
         return carry
 
-    def greet_ring(step, carry):
-        spot = (place + step) % RING
-
-        @pl.when(spot > place)
-        def _():
-            pl.semaphore_signal(barrier, inc=1, device_id=at(spot), device_id_type=MESH)
-
+    def greet_ring(spot, carry):
+        pl.semaphore_signal(barrier, inc=1, device_id=at(spot), device_id_type=MESH)
         return carry
 
-    def answer_ring(step, carry):
-        spot = (place + step) % RING
-
-        @pl.when(spot < place)
-        def _():
-            pl.semaphore_signal(
-                ready.at[place], inc=1, device_id=at(spot), device_id_type=MESH
-            )
-
+    def answer_ring(spot, carry):
+        pl.semaphore_signal(ready.at[place], inc=1, device_id=at(spot), device_id_type=MESH)
         return carry
 
     lax.fori_loop(1, PEERS, greet_plane, 0)
-    lax.fori_loop(1, RING, greet_ring, 0)
-
-    load_steer = pltpu.make_async_copy(steer_all.at[half], steer, table_sem.at[0])
-    load_steer.start()
-    load_early = pltpu.make_async_copy(early_all.at[sector % 4], early, table_sem.at[1])
-    load_early.start()
+    lax.fori_loop(place + 1, RING, greet_ring, 0)
+
+    for load in loads[:3]:
+        load.wait()
 
     for part in range(2):
         spread[part] = raw[part].astype(jnp.float32).reshape(RADIX * OWN, RADIX)
@@ -201,6 +221,7 @@
             twisted[rows, :RADIX] = (real * cosine - imag * sine).astype(jnp.bfloat16)
             twisted[rows, RADIX:] = (real * sine + imag * cosine).astype(jnp.bfloat16)
     lane = lax.broadcasted_iota(jnp.int32, (RADIX // HALVES, RADIX), 1)
+    upper = lax.broadcasted_iota(jnp.int32, (8, RADIX), 0) < 4
 
     def range_gates(side):
         count = RADIX // HALVES
@@ -236,12 +257,12 @@
             blocks[side, :, :, late * RADIX : (late + 1) * RADIX] = rows[:, late]
 
     def plane_copy(side, step):
-        other = (peer + step) % PEERS
+        other = lax.rem(peer + step, PEERS)
         return pltpu.make_async_remote_copy(
             src_ref=blocks.at[side, other],
             dst_ref=pulses.at[side, peer],
-            send_sem=plane_send.at[side, step],
-            recv_sem=plane_recv.at[side, step],
+            send_sem=plane_send.at[side],
+            recv_sem=plane_recv.at[side],
             device_id={"gate": half * PEERS + other},
             device_id_type=MESH,
         )
@@ -255,11 +276,10 @@
         pulses[side, peer] = blocks[side, peer]
 
     def plane_waits(side):
-        def wait(step, carry):
-            plane_copy(side, step).wait()
-            return carry
-
-        lax.fori_loop(1, PEERS, wait, 0)
+        others = pl.ds(0, PEERS - 1)
+        pltpu.make_async_copy(
+            blocks.at[side, others], pulses.at[side, others], plane_recv.at[side]
+        ).wait()
 
     def beam_sums(side):
         beams = jnp.dot(
@@ -268,53 +288,85 @@
             preferred_element_type=jnp.float32,
         )
         for q in range(N_SUB):
-            window = beams[q * ROWS : (q + 1) * ROWS]
-            outgoing[side, q] = jnp.concatenate(
-                [window[:, :RADIX], window[:, RADIX:]], axis=0
+            window = beams[q * ROWS : (q + 1) * ROWS].reshape(ROWS // 8, 8, BLOCK)
+            shared = WIDTHS[q % 4] // 4
+            base = (side * N_SUB + q) * TILES
+            for t in range(shared):
+                for lanes in range(2):
+                    outgoing[base + 2 * t + lanes] = window[
+                        t, :, lanes * RADIX : (lanes + 1) * RADIX
+                    ].astype(jnp.bfloat16)
+            outgoing[base + 2 * shared] = jnp.where(
+                upper, window[shared, :, :RADIX], pltpu.roll(window[shared, :, RADIX:], 4, 0)
             ).astype(jnp.bfloat16)
 
-    def ring_copy(step):
-        spot = (place + step) % RING
+    def ring_copy(spot, tiles):
+        there = lax.rem(spot, N_SUB)
+        source = (spot - there + swapped_bits(there)) * TILES
         return pltpu.make_async_remote_copy(
-            src_ref=outgoing.at[spot // N_SUB, swapped_bits(spot % N_SUB)],
-            dst_ref=incoming.at[half, sub],
-            send_sem=ring_send.at[step],
-            recv_sem=ring_recv.at[step],
+            src_ref=outgoing.at[pl.ds(source, tiles)],
+            dst_ref=incoming.at[pl.ds(place * TILES, tiles)],
+            send_sem=ring_send,
+            recv_sem=ring_recv.at[lax.div(sub, 4)],
             device_id=at(spot),
             device_id_type=MESH,
         )
 
+    def own_copy(tiles):
+        return pltpu.make_async_copy(
+            outgoing.at[pl.ds((half * N_SUB + sector) * TILES, tiles)],
+            incoming.at[pl.ds(place * TILES, tiles)],
+            ring_recv.at[lax.div(sub, 4)],
+        )
+
+    def on_edge(there):
+        _, middle, high = bits(there)
+        return middle == high
+
+    def by_size(there, act):
+        edge = on_edge(there)
+
+        @pl.when(edge)
+        def _():
+            act(EDGE_TILES)
+
+        @pl.when(jnp.logical_not(edge))
+        def _():
+            act(TILES)
+
     def ring_starts(side):
         def start(turn, carry):
-            distance = RING // 2 - (turn + 1) // 2
-            step = jnp.where(turn % 2 == 0, RING - distance, distance)
-            spot = (place + step) % RING
-
-            @pl.when(spot // N_SUB == side)
+            distance = RING // 2 - lax.div(turn + 1, 2)
+            step = jnp.where(lax.rem(turn, 2) == 0, RING - distance, distance)
+            spot = lax.rem(place + step, RING)
+
+            @pl.when(lax.div(spot, N_SUB) == side)
             def _():
                 @pl.when(spot > place)
                 def _():
                     pl.semaphore_wait(ready.at[spot], 1)
 
-                ring_copy(step).start()
+                by_size(lax.rem(spot, N_SUB), lambda tiles: ring_copy(spot, tiles).start())
 
             return carry
 
         lax.fori_loop(0, RING - 1, start, 0)
 
+    loads[3].wait()
     range_gates(0)
     pl.semaphore_wait(barrier, PEERS - 1 + place)
     plane_starts(0)
-    lax.fori_loop(1, RING, answer_ring, 0)
+    lax.fori_loop(0, place, answer_ring, 0)
     range_gates(1)
     plane_starts(1)
-    load_steer.wait()
-    load_early.wait()
+    loads[4].wait()
     for side in range(HALVES):
         plane_waits(side)
         beam_sums(side)
         ring_starts(side)
-    incoming[half, sub] = outgoing[half, sector]
+    by_size(sub, lambda tiles: own_copy(tiles).start())
+    for load in loads[5:]:
+        load.wait()
 
     position = (
         gate * BLOCK + lax.broadcasted_iota(jnp.int32, (1, BLOCK), 1) + SAMPLES
@@ -323,20 +375,37 @@
     gate_cos = jnp.cos(phase)
     gate_sin = jnp.sin(phase)
 
-    def ring_wait(step, carry):
-        ring_copy(step).wait()
-        return carry
-
-    lax.fori_loop(1, RING, ring_wait, 0)
+    edge = on_edge(sub)
+
+    def taken(late, tiles):
+        count = pl.ds(0, N_SUB * tiles)
+        pltpu.make_async_copy(outgoing.at[count], incoming.at[count], ring_recv.at[late]).wait()
 
     total = None
     for late in range(2):
+        by_size(sub, functools.partial(taken, late))
         children = []
         for s in range(4 * late, 4 * late + 4):
-            both = incoming[0, s].astype(jnp.float32) + incoming[1, s].astype(jnp.float32)
-            children.append(
-                jnp.concatenate([both[:ROWS], both[ROWS:]], axis=1).astype(jnp.bfloat16)
-            )
+            both = [
+                incoming[pl.ds((side * N_SUB + s) * TILES, TILES)].astype(jnp.float32)
+                for side in range(HALVES)
+            ]
+            both = both[0] + both[1]
+            paired = both[: TILES - 1].reshape(TILES // 2, 2, 8, RADIX)
+            lanes = []
+            for side in range(2):
+                last_tile = both[TILES - 1]
+                edge_tile = both[EDGE_TILES - 1]
+                if side == 1:
+                    last_tile = pltpu.roll(last_tile, 4, 0)
+                    edge_tile = pltpu.roll(edge_tile, 4, 0)
+                tiles = [
+                    paired[: TILES // 2 - 1, side],
+                    jnp.where(edge, edge_tile, paired[TILES // 2 - 1, side])[None],
+                    jnp.where(edge, 0.0, last_tile)[None],
+                ]
+                lanes.append(jnp.concatenate(tiles, axis=0).reshape(ROWS, RADIX))
+            children.append(jnp.concatenate(lanes, axis=1).astype(jnp.bfloat16))
         level_two = jnp.dot(
             early[...], jnp.concatenate(children, axis=0), preferred_element_type=jnp.float32
         ).astype(jnp.bfloat16)
@@ -350,6 +419,18 @@
     imag = total[ANGLES:]
     image[0] = (real * gate_cos - imag * gate_sin).astype(jnp.bfloat16)
     image[1] = (real * gate_sin + imag * gate_cos).astype(jnp.bfloat16)
+
+    for side in range(HALVES):
+        others = pl.ds(0, PEERS - 1)
+        pltpu.make_async_copy(
+            blocks.at[side, others], pulses.at[side, others], plane_send.at[side]
+        ).wait()
+
+    def sent(tiles):
+        count = pl.ds(0, ALL_TILES - tiles)
+        pltpu.make_async_copy(outgoing.at[count], incoming.at[count], ring_send).wait()
+
+    by_size(sub, sent)
 
 
 def per_device(raw_echo, delays):
@@ -361,9 +442,14 @@
     return pl.pallas_call(
         kernel,
         out_shape=jax.ShapeDtypeStruct((2, ANGLES, BLOCK), jnp.bfloat16),
-        in_specs=[pl.BlockSpec(memory_space=pltpu.SMEM), vmem, vmem, vmem, vmem, vmem, hbm, hbm],
+        in_specs=[pl.BlockSpec(memory_space=pltpu.SMEM)] + [hbm] * 7,
         out_specs=vmem,
         scratch_shapes=[
+            pltpu.VMEM((2, RADIX, OWN, RADIX), jnp.bfloat16),
+            pltpu.VMEM(dft.shape, jnp.bfloat16),
+            pltpu.VMEM(dft_half.shape, jnp.bfloat16),
+            pltpu.VMEM((2, RADIX, RADIX), jnp.float32),
+            pltpu.VMEM(last.shape, jnp.bfloat16),
             pltpu.VMEM((N_SUB * ROWS, PEERS * 2 * OWN), jnp.bfloat16),
             pltpu.VMEM((ANGLES, 4 * ROWS), jnp.bfloat16),
             pltpu.VMEM((2, RADIX * OWN, RADIX), jnp.float32),
@@ -372,14 +458,14 @@
             pltpu.VMEM((2, HELD, RADIX), jnp.float32),
             pltpu.VMEM((HALVES, PEERS, 2 * OWN, BLOCK), jnp.bfloat16),
             pltpu.VMEM((HALVES, PEERS, 2 * OWN, BLOCK), jnp.bfloat16),
-            pltpu.VMEM((HALVES, N_SUB, 2 * ROWS, RADIX), jnp.bfloat16),
-            pltpu.VMEM((HALVES, N_SUB, 2 * ROWS, RADIX), jnp.bfloat16),
+            pltpu.VMEM((RING * TILES, 8, RADIX), jnp.bfloat16),
+            pltpu.VMEM((RING * TILES, 8, RADIX), jnp.bfloat16),
             pltpu.SemaphoreType.REGULAR((RING,)),
+            pltpu.SemaphoreType.DMA((7,)),
+            pltpu.SemaphoreType.DMA((HALVES,)),
+            pltpu.SemaphoreType.DMA((HALVES,)),
+            pltpu.SemaphoreType.DMA,
             pltpu.SemaphoreType.DMA((2,)),
-            pltpu.SemaphoreType.DMA((HALVES, PEERS)),
-            pltpu.SemaphoreType.DMA((HALVES, PEERS)),
-            pltpu.SemaphoreType.DMA((RING,)),
-            pltpu.SemaphoreType.DMA((RING,)),
         ],
         compiler_params=pltpu.CompilerParams(collective_id=0, has_side_effects=True),
         name="image_formation",

time: 64.4 us -> 59.2 us (0.919)
  Pallas kernels: 62.5 us -> 57.3 us
    pallas_call x1, Pallas kernels: 62.5 us -> 57.3 us  [per_device(): pl.pallas_call(kernel, out_shape=jax.ShapeDtypeStruct((2, ANGLES, BLOCK),...]
where the time goes in v3:
time: 59.2 us; the launch traced here: 59 us
  Pallas kernels  57.3 us (97%)
  local copies, waits for them, and re-layouts  1.67 us (3%)
    pallas_call x1, Pallas kernels, per_device(): pl.pallas_call(kernel, out_shape=jax.ShapeDtypeStruct((2, ANGLES, BLOCK),...  57.3 us
    unnamed x1, local copies, waits for them, and re-layouts  1.67 us

profile of v3, /device:TPU:1, one launch (start us, length us, event | category | flops | bytes accessed | tf_op | source)
XLA Modules:
  0.0 59.0 jit_solution(6310065835623051597)
XLA Ops:
  0.0 57.3 %image_formation.1 = bf16[2,256,256]{2,1,0:T(8,128)(2,1)} custom-call(s32[8]{0:T(128)} %delays.1, bf16[2,128,8,128]{3,2,1,0:T(8,128)(2,1)} %bitcast.3, bf16[256,256]{1,0:T(8,128)(2,1)} %constant.12.clone.dft_in, bf16[2,144,256]{2,1,0:T(8,128)(2,1)} %constant.13.clone.dft_half_in, f32[2,128,128]{2,1,0:T(8,128)} %constant.14.clone.twiddle_in, ...), custom_call_target="tpu_custom_call" | custom-call | tf_op jit(solution)/shard_map/image_formation/pallas_call | solution.py:442
  57.3 1.7 %copy.10 = bf16[2,256,256]{2,1,0:T(8,128)(2,1)} copy(bf16[2,256,256]{2,1,0:T(8,128)(2,1)} %image_formation.1) | data formatting | bytes 524288

commit v4 on v3

--- a/solution.py
+++ b/solution.py
@@ -25,6 +25,7 @@
 ROWS = 88
 TILES = 21
 EDGE_TILES = 19
+FIRST_TILES = 10
 ALL_TILES = N_SUB * (TILES + EDGE_TILES)
 HELD = RADIX // HALVES + 8
 STARTS = (0, 26, 60, 90)
@@ -142,6 +143,7 @@
     rolled,
     blocks,
     pulses,
+    kept,
     outgoing,
     incoming,
     ready,
@@ -254,68 +256,76 @@
         ).astype(jnp.bfloat16)
         rows = rows.reshape(PEERS, 2, 2 * OWN, RADIX)
         for late in range(2):
-            blocks[side, :, :, late * RADIX : (late + 1) * RADIX] = rows[:, late]
-
-    def plane_copy(side, step):
+            blocks[late, side] = rows[:, late]
+
+    def plane_copy(chunk, step):
         other = lax.rem(peer + step, PEERS)
         return pltpu.make_async_remote_copy(
-            src_ref=blocks.at[side, other],
-            dst_ref=pulses.at[side, peer],
-            send_sem=plane_send.at[side],
-            recv_sem=plane_recv.at[side],
+            src_ref=blocks.at[chunk, :, other],
+            dst_ref=pulses.at[chunk, :, peer],
+            send_sem=plane_send.at[chunk],
+            recv_sem=plane_recv.at[chunk],
             device_id={"gate": half * PEERS + other},
             device_id_type=MESH,
         )
 
-    def plane_starts(side):
+    def plane_starts(chunk):
         def start(step, carry):
-            plane_copy(side, step).start()
+            plane_copy(chunk, step).start()
             return carry
 
         lax.fori_loop(1, PEERS, start, 0)
-        pulses[side, peer] = blocks[side, peer]
-
-    def plane_waits(side):
+        for side in range(HALVES):
+            pulses[chunk, side, peer] = blocks[chunk, side, peer]
+
+    def plane_wait(chunk, semaphores):
         others = pl.ds(0, PEERS - 1)
         pltpu.make_async_copy(
-            blocks.at[side, others], pulses.at[side, others], plane_recv.at[side]
+            blocks.at[chunk, :, others], pulses.at[chunk, :, others], semaphores.at[chunk]
         ).wait()
 
-    def beam_sums(side):
+    def beam_sums(chunk):
         beams = jnp.dot(
             steer[...],
-            pulses[side].reshape(PEERS * 2 * OWN, BLOCK),
+            jnp.concatenate(
+                [pulses[chunk, side].reshape(PEERS * 2 * OWN, RADIX) for side in range(HALVES)],
+                axis=1,
+            ),
             preferred_element_type=jnp.float32,
         )
-        for q in range(N_SUB):
-            window = beams[q * ROWS : (q + 1) * ROWS].reshape(ROWS // 8, 8, BLOCK)
-            shared = WIDTHS[q % 4] // 4
-            base = (side * N_SUB + q) * TILES
-            for t in range(shared):
-                for lanes in range(2):
-                    outgoing[base + 2 * t + lanes] = window[
-                        t, :, lanes * RADIX : (lanes + 1) * RADIX
-                    ].astype(jnp.bfloat16)
-            outgoing[base + 2 * shared] = jnp.where(
-                upper, window[shared, :, :RADIX], pltpu.roll(window[shared, :, RADIX:], 4, 0)
-            ).astype(jnp.bfloat16)
-
-    def ring_copy(spot, tiles):
+        for side in range(HALVES):
+            for q in range(N_SUB):
+                window = beams[q * ROWS : (q + 1) * ROWS, side * RADIX : (side + 1) * RADIX]
+                window = window.reshape(ROWS // 8, 8, RADIX)
+                shared = WIDTHS[q % 4] // 4
+                slot = side * N_SUB + q
+                base = slot * TILES + chunk * FIRST_TILES
+                for t in range(shared):
+                    outgoing[base + t] = window[t].astype(jnp.bfloat16)
+                if chunk == 0:
+                    kept[slot] = window[shared]
+                else:
+                    outgoing[base + shared] = jnp.where(
+                        upper, kept[slot], pltpu.roll(window[shared], 4, 0)
+                    ).astype(jnp.bfloat16)
+
+    def ring_copy(chunk, spot, tiles):
         there = lax.rem(spot, N_SUB)
-        source = (spot - there + swapped_bits(there)) * TILES
+        source = (spot - there + swapped_bits(there)) * TILES + chunk * FIRST_TILES
         return pltpu.make_async_remote_copy(
             src_ref=outgoing.at[pl.ds(source, tiles)],
-            dst_ref=incoming.at[pl.ds(place * TILES, tiles)],
+            dst_ref=incoming.at[pl.ds(place * TILES + chunk * FIRST_TILES, tiles)],
             send_sem=ring_send,
             recv_sem=ring_recv.at[lax.div(sub, 4)],
             device_id=at(spot),
             device_id_type=MESH,
         )
 
-    def own_copy(tiles):
+    def own_copy(chunk, tiles):
+        source = (half * N_SUB + sector) * TILES + chunk * FIRST_TILES
         return pltpu.make_async_copy(
-            outgoing.at[pl.ds((half * N_SUB + sector) * TILES, tiles)],
-            incoming.at[pl.ds(place * TILES, tiles)],
+            outgoing.at[pl.ds(source, tiles)],
+            incoming.at[pl.ds(place * TILES + chunk * FIRST_TILES, tiles)],
             ring_recv.at[lax.div(sub, 4)],
         )
 
@@ -323,48 +333,46 @@
         _, middle, high = bits(there)
         return middle == high
 
-    def by_size(there, act):
+    def by_size(there, small, large, act):
         edge = on_edge(there)
 
         @pl.when(edge)
         def _():
-            act(EDGE_TILES)
+            act(small)
 
         @pl.when(jnp.logical_not(edge))
         def _():
-            act(TILES)
-
-    def ring_starts(side):
-        def start(turn, carry):
-            distance = RING // 2 - lax.div(turn + 1, 2)
-            step = jnp.where(lax.rem(turn, 2) == 0, RING - distance, distance)
-            spot = lax.rem(place + step, RING)
-
-            @pl.when(lax.div(spot, N_SUB) == side)
-            def _():
-                @pl.when(spot > place)
-                def _():
-                    pl.semaphore_wait(ready.at[spot], 1)
-
-                by_size(lax.rem(spot, N_SUB), lambda tiles: ring_copy(spot, tiles).start())
-
+            act(large)
+
+    def ring_starts(chunk):
+        sizes = EDGE_WINDOW // 4 + chunk, WINDOW // 4 + chunk
+
+        def start(spot, carry):
+            there = lax.rem(spot, N_SUB)
+            by_size(there, *sizes, lambda tiles: ring_copy(chunk, spot, tiles).start())
             return carry
 
-        lax.fori_loop(0, RING - 1, start, 0)
+        def start_later(spot, carry):
+            if chunk == 0:
+                pl.semaphore_wait(ready.at[spot], 1)
+            return start(spot, carry)
+
+        lax.fori_loop(0, place, start, 0)
+        lax.fori_loop(place + 1, RING, start_later, 0)
+        by_size(sub, *sizes, lambda tiles: own_copy(chunk, tiles).start())
 
     loads[3].wait()
-    range_gates(0)
+    for side in range(HALVES):
+        range_gates(side)
     pl.semaphore_wait(barrier, PEERS - 1 + place)
     plane_starts(0)
     lax.fori_loop(0, place, answer_ring, 0)
-    range_gates(1)
     plane_starts(1)
     loads[4].wait()
-    for side in range(HALVES):
-        plane_waits(side)
-        beam_sums(side)
-        ring_starts(side)
-    by_size(sub, lambda tiles: own_copy(tiles).start())
+    for chunk in range(2):
+        plane_wait(chunk, plane_recv)
+        beam_sums(chunk)
+        ring_starts(chunk)
     for load in loads[5:]:
         load.wait()
 
@@ -383,7 +391,7 @@
 
     total = None
     for late in range(2):
-        by_size(sub, functools.partial(taken, late))
+        by_size(sub, EDGE_TILES, TILES, functools.partial(taken, late))
         children = []
         for s in range(4 * late, 4 * late + 4):
             both = [
@@ -391,18 +399,16 @@
                 for side in range(HALVES)
             ]
             both = both[0] + both[1]
-            paired = both[: TILES - 1].reshape(TILES // 2, 2, 8, RADIX)
             lanes = []
-            for side in range(2):
-                last_tile = both[TILES - 1]
-                edge_tile = both[EDGE_TILES - 1]
-                if side == 1:
-                    last_tile = pltpu.roll(last_tile, 4, 0)
-                    edge_tile = pltpu.roll(edge_tile, 4, 0)
+            for chunk in range(2):
+                ends = [both[EDGE_TILES], both[TILES - 1]]
+                if chunk == 1:
+                    ends = [pltpu.roll(end, 4, 0) for end in ends]
+                first = chunk * FIRST_TILES
                 tiles = [
-                    paired[: TILES // 2 - 1, side],
-                    jnp.where(edge, edge_tile, paired[TILES // 2 - 1, side])[None],
-                    jnp.where(edge, 0.0, last_tile)[None],
+                    both[first : first + FIRST_TILES - 1],
+                    jnp.where(edge, ends[0], both[first + FIRST_TILES - 1])[None],
+                    jnp.where(edge, 0.0, ends[1])[None],
                 ]
                 lanes.append(jnp.concatenate(tiles, axis=0).reshape(ROWS, RADIX))
             children.append(jnp.concatenate(lanes, axis=1).astype(jnp.bfloat16))
@@ -420,17 +426,14 @@
     image[0] = (real * gate_cos - imag * gate_sin).astype(jnp.bfloat16)
     image[1] = (real * gate_sin + imag * gate_cos).astype(jnp.bfloat16)
 
-    for side in range(HALVES):
-        others = pl.ds(0, PEERS - 1)
-        pltpu.make_async_copy(
-            blocks.at[side, others], pulses.at[side, others], plane_send.at[side]
-        ).wait()
+    for chunk in range(2):
+        plane_wait(chunk, plane_send)
 
     def sent(tiles):
         count = pl.ds(0, ALL_TILES - tiles)
         pltpu.make_async_copy(outgoing.at[count], incoming.at[count], ring_send).wait()
 
-    by_size(sub, sent)
+    by_size(sub, EDGE_TILES, TILES, sent)
 
 
 def per_device(raw_echo, delays):
@@ -441,7 +444,7 @@
     hbm = pl.BlockSpec(memory_space=pl.ANY)
     return pl.pallas_call(
         kernel,
-        out_shape=jax.ShapeDtypeStruct((2, ANGLES, BLOCK), jnp.bfloat16),
+        out_shape=pltpu.VMEM((2, ANGLES, BLOCK), jnp.bfloat16),
         in_specs=[pl.BlockSpec(memory_space=pltpu.SMEM)] + [hbm] * 7,
         out_specs=vmem,
         scratch_shapes=[
@@ -456,8 +459,9 @@
             pltpu.VMEM((2 * RADIX, OWN * RADIX), jnp.bfloat16),
             pltpu.VMEM((OWN * RADIX, 2 * RADIX), jnp.bfloat16),
             pltpu.VMEM((2, HELD, RADIX), jnp.float32),
-            pltpu.VMEM((HALVES, PEERS, 2 * OWN, BLOCK), jnp.bfloat16),
-            pltpu.VMEM((HALVES, PEERS, 2 * OWN, BLOCK), jnp.bfloat16),
+            pltpu.VMEM((2, HALVES, PEERS, 2 * OWN, RADIX), jnp.bfloat16),
+            pltpu.VMEM((2, HALVES, PEERS, 2 * OWN, RADIX), jnp.bfloat16),
+            pltpu.VMEM((RING, 8, RADIX), jnp.float32),
             pltpu.VMEM((RING * TILES, 8, RADIX), jnp.bfloat16),
             pltpu.VMEM((RING * TILES, 8, RADIX), jnp.bfloat16),
             pltpu.SemaphoreType.REGULAR((RING,)),

time: 59.2 us -> 54 us (0.912)
  the two profiles are of different devices: /device:TPU:1 before, /device:TPU:161 now
where the time goes in v4:
time: 54 us; the launch traced here: 53.8 us
  Pallas kernels  53.1 us (98%)
  local copies, waits for them, and re-layouts  0.71 us (1%)
    pallas_call x1, Pallas kernels, per_device(): pl.pallas_call(kernel, out_shape=pltpu.VMEM((2, ANGLES, BLOCK), jnp.bfloa...  53.1 us

profile of v4, /device:TPU:161, one launch (start us, length us, event | category | flops | bytes accessed | tf_op | source)
XLA Modules:
  0.0 53.8 jit_solution(6017057666047136428)
XLA Ops:
  0.0 53.1 %image_formation.1 = bf16[2,256,256]{2,1,0:T(8,128)(2,1)S(1)} custom-call(s32[8]{0:T(128)} %delays.1, bf16[2,128,8,128]{3,2,1,0:T(8,128)(2,1)} %bitcast.3, bf16[256,256]{1,0:T(8,128)(2,1)} %constant.12.clone.dft_in, bf16[2,144,256]{2,1,0:T(8,128)(2,1)} %constant.13.clone.dft_half_in, f32[2,128,128]{2,1,0:T(8,128)} %constant.14.clone.twiddle_in, ...), custom_call_target="tpu_custom_call" | custom-call | tf_op jit(solution)/shard_map/image_formation/pallas_call | solution.py:445
  53.1 0.7 %copy.10 = bf16[2,256,256]{2,1,0:T(8,128)(2,1)} copy(bf16[2,256,256]{2,1,0:T(8,128)(2,1)S(1)} %image_formation.1) | data formatting | bytes 524288

commit v5 on v3

--- a/solution.py
+++ b/solution.py
@@ -335,22 +335,17 @@
             act(TILES)
 
     def ring_starts(side):
-        def start(turn, carry):
-            distance = RING // 2 - lax.div(turn + 1, 2)
-            step = jnp.where(lax.rem(turn, 2) == 0, RING - distance, distance)
-            spot = lax.rem(place + step, RING)
-
-            @pl.when(lax.div(spot, N_SUB) == side)
-            def _():
-                @pl.when(spot > place)
-                def _():
-                    pl.semaphore_wait(ready.at[spot], 1)
-
-                by_size(lax.rem(spot, N_SUB), lambda tiles: ring_copy(spot, tiles).start())
-
+        def start(spot, carry):
+            by_size(lax.rem(spot, N_SUB), lambda tiles: ring_copy(spot, tiles).start())
             return carry
 
-        lax.fori_loop(0, RING - 1, start, 0)
+        def start_later(spot, carry):
+            pl.semaphore_wait(ready.at[spot], 1)
+            return start(spot, carry)
+
+        first = side * N_SUB
+        lax.fori_loop(first, jnp.minimum(place, first + N_SUB), start, 0)
+        lax.fori_loop(jnp.maximum(place + 1, first), first + N_SUB, start_later, 0)
 
     loads[3].wait()
     range_gates(0)
@@ -441,7 +436,7 @@
     hbm = pl.BlockSpec(memory_space=pl.ANY)
     return pl.pallas_call(
         kernel,
-        out_shape=jax.ShapeDtypeStruct((2, ANGLES, BLOCK), jnp.bfloat16),
+        out_shape=pltpu.VMEM((2, ANGLES, BLOCK), jnp.bfloat16),
         in_specs=[pl.BlockSpec(memory_space=pltpu.SMEM)] + [hbm] * 7,
         out_specs=vmem,
         scratch_shapes=[

time: 59.2 us -> 53.9 us (0.910)
  the two profiles are of different devices: /device:TPU:1 before, /device:TPU:193 now
where the time goes in v5:
time: 53.9 us; the launch traced here: 53.8 us
  Pallas kernels  53.1 us (99%)
  local copies, waits for them, and re-layouts  0.71 us (1%)
    pallas_call x1, Pallas kernels, per_device(): pl.pallas_call(kernel, out_shape=pltpu.VMEM((2, ANGLES, BLOCK), jnp.bfloa...  53.1 us

profile of v5, /device:TPU:193, one launch (start us, length us, event | category | flops | bytes accessed | tf_op | source)
XLA Modules:
  0.0 53.8 jit_solution(7981334310406024432)
XLA Ops:
  0.0 53.1 %image_formation.1 = bf16[2,256,256]{2,1,0:T(8,128)(2,1)S(1)} custom-call(s32[8]{0:T(128)} %delays.1, bf16[2,128,8,128]{3,2,1,0:T(8,128)(2,1)} %bitcast.3, bf16[256,256]{1,0:T(8,128)(2,1)} %constant.12.clone.dft_in, bf16[2,144,256]{2,1,0:T(8,128)(2,1)} %constant.13.clone.dft_half_in, f32[2,128,128]{2,1,0:T(8,128)} %constant.14.clone.twiddle_in, ...), custom_call_target="tpu_custom_call" | custom-call | tf_op jit(solution)/shard_map/image_formation/pallas_call | solution.py:437
  53.1 0.7 %copy.10 = bf16[2,256,256]{2,1,0:T(8,128)(2,1)} copy(bf16[2,256,256]{2,1,0:T(8,128)(2,1)S(1)} %image_formation.1) | data formatting | bytes 524288

commit v6 on v4

--- a/solution.py
+++ b/solution.py
@@ -18,6 +18,7 @@
 HALVES = 2
 PEERS = 32
 RING = HALVES * N_SUB
+STAGES = 3
 OWN = 8
 BLOCK = 256
 WINDOW = 42
@@ -258,55 +259,60 @@
         for late in range(2):
             blocks[late, side] = rows[:, late]
 
-    def plane_copy(chunk, step):
+    def lanes_of(stage):
+        return pl.ds(stage, 1) if stage < 2 else pl.ds(0, 2)
+
+    def plane_copy(stage, step):
         other = lax.rem(peer + step, PEERS)
         return pltpu.make_async_remote_copy(
-            src_ref=blocks.at[chunk, :, other],
-            dst_ref=pulses.at[chunk, :, peer],
-            send_sem=plane_send.at[chunk],
-            recv_sem=plane_recv.at[chunk],
+            src_ref=blocks.at[lanes_of(stage), stage // 2, other],
+            dst_ref=pulses.at[lanes_of(stage), stage // 2, peer],
+            send_sem=plane_send.at[stage],
+            recv_sem=plane_recv.at[stage],
             device_id={"gate": half * PEERS + other},
             device_id_type=MESH,
         )
 
-    def plane_starts(chunk):
+    def plane_starts(stage):
         def start(step, carry):
-            plane_copy(chunk, step).start()
+            plane_copy(stage, step).start()
             return carry
 
         lax.fori_loop(1, PEERS, start, 0)
-        for side in range(HALVES):
-            pulses[chunk, side, peer] = blocks[chunk, side, peer]
-
-    def plane_wait(chunk, semaphores):
+        for chunk in (stage,) if stage < 2 else (0, 1):
+            pulses[chunk, stage // 2, peer] = blocks[chunk, stage // 2, peer]
+
+    def plane_wait(stage, semaphores):
         others = pl.ds(0, PEERS - 1)
         pltpu.make_async_copy(
-            blocks.at[chunk, :, others], pulses.at[chunk, :, others], semaphores.at[chunk]
+            blocks.at[lanes_of(stage), stage // 2, others],
+            pulses.at[lanes_of(stage), stage // 2, others],
+            semaphores.at[stage],
         ).wait()
 
-    def beam_sums(chunk):
+    def beam_sums(stage):
+        side = stage // 2
+        chunks = (stage,) if stage < 2 else (0, 1)
         beams = jnp.dot(
             steer[...],
             jnp.concatenate(
-                [pulses[chunk, side].reshape(PEERS * 2 * OWN, RADIX) for side in range(HALVES)],
-                axis=1,
+                [pulses[chunk, side].reshape(PEERS * 2 * OWN, RADIX) for chunk in chunks], axis=1
             ),
             preferred_element_type=jnp.float32,
         )
-        for side in range(HALVES):
+        for place_in, chunk in enumerate(chunks):
             for q in range(N_SUB):
-                window = beams[q * ROWS : (q + 1) * ROWS, side * RADIX : (side + 1) * RADIX]
+                window = beams[q * ROWS : (q + 1) * ROWS, place_in * RADIX : (place_in + 1) * RADIX]
                 window = window.reshape(ROWS // 8, 8, RADIX)
                 shared = WIDTHS[q % 4] // 4
-                slot = side * N_SUB + q
-                base = slot * TILES + chunk * FIRST_TILES
+                base = (side * N_SUB + q) * TILES + chunk * FIRST_TILES
                 for t in range(shared):
                     outgoing[base + t] = window[t].astype(jnp.bfloat16)
                 if chunk == 0:
-                    kept[slot] = window[shared]
+                    kept[q] = window[shared]
                 else:
                     outgoing[base + shared] = jnp.where(
-                        upper, kept[slot], pltpu.roll(window[shared], 4, 0)
+                        upper, kept[q], pltpu.roll(window[shared], 4, 0)
                     ).astype(jnp.bfloat16)
 
     def ring_copy(chunk, spot, tiles):
@@ -344,35 +350,51 @@
         def _():
             act(large)
 
-    def ring_starts(chunk):
-        sizes = EDGE_WINDOW // 4 + chunk, WINDOW // 4 + chunk
+    def ring_starts(stage):
+        side = stage // 2
+        chunks = (stage,) if stage < 2 else (0, 1)
+
+        def act(there, copy):
+            def small(_):
+                for chunk in chunks:
+                    copy(chunk, EDGE_WINDOW // 4 + chunk).start()
+
+            def large(_):
+                for chunk in chunks:
+                    copy(chunk, WINDOW // 4 + chunk).start()
+
+            by_size(there, 0, 1, lambda size: (small, large)[size](None))
 
         def start(spot, carry):
-            there = lax.rem(spot, N_SUB)
-            by_size(there, *sizes, lambda tiles: ring_copy(chunk, spot, tiles).start())
+            act(lax.rem(spot, N_SUB), lambda chunk, tiles: ring_copy(chunk, spot, tiles))
             return carry
 
         def start_later(spot, carry):
-            if chunk == 0:
+            if stage != 1:
                 pl.semaphore_wait(ready.at[spot], 1)
             return start(spot, carry)
 
-        lax.fori_loop(0, place, start, 0)
-        lax.fori_loop(place + 1, RING, start_later, 0)
-        by_size(sub, *sizes, lambda tiles: own_copy(chunk, tiles).start())
+        first = side * N_SUB
+        lax.fori_loop(first, jnp.minimum(place, first + N_SUB), start, 0)
+        lax.fori_loop(jnp.maximum(place + 1, first), first + N_SUB, start_later, 0)
+
+        @pl.when(half == side)
+        def _():
+            act(sub, own_copy)
 
     loads[3].wait()
-    for side in range(HALVES):
-        range_gates(side)
+    range_gates(0)
     pl.semaphore_wait(barrier, PEERS - 1 + place)
+    lax.fori_loop(0, place, answer_ring, 0)
     plane_starts(0)
-    lax.fori_loop(0, place, answer_ring, 0)
     plane_starts(1)
+    range_gates(1)
+    plane_starts(2)
     loads[4].wait()
-    for chunk in range(2):
-        plane_wait(chunk, plane_recv)
-        beam_sums(chunk)
-        ring_starts(chunk)
+    for stage in range(STAGES):
+        plane_wait(stage, plane_recv)
+        beam_sums(stage)
+        ring_starts(stage)
     for load in loads[5:]:
         load.wait()
 
@@ -426,8 +448,8 @@
     image[0] = (real * gate_cos - imag * gate_sin).astype(jnp.bfloat16)
     image[1] = (real * gate_sin + imag * gate_cos).astype(jnp.bfloat16)
 
-    for chunk in range(2):
-        plane_wait(chunk, plane_send)
+    for stage in range(STAGES):
+        plane_wait(stage, plane_send)
 
     def sent(tiles):
         count = pl.ds(0, ALL_TILES - tiles)
@@ -461,13 +483,13 @@
             pltpu.VMEM((2, HELD, RADIX), jnp.float32),
             pltpu.VMEM((2, HALVES, PEERS, 2 * OWN, RADIX), jnp.bfloat16),
             pltpu.VMEM((2, HALVES, PEERS, 2 * OWN, RADIX), jnp.bfloat16),
-            pltpu.VMEM((RING, 8, RADIX), jnp.float32),
+            pltpu.VMEM((N_SUB, 8, RADIX), jnp.float32),
             pltpu.VMEM((RING * TILES, 8, RADIX), jnp.bfloat16),
             pltpu.VMEM((RING * TILES, 8, RADIX), jnp.bfloat16),
             pltpu.SemaphoreType.REGULAR((RING,)),
             pltpu.SemaphoreType.DMA((7,)),
-            pltpu.SemaphoreType.DMA((HALVES,)),
-            pltpu.SemaphoreType.DMA((HALVES,)),
+            pltpu.SemaphoreType.DMA((STAGES,)),
+            pltpu.SemaphoreType.DMA((STAGES,)),
             pltpu.SemaphoreType.DMA,
             pltpu.SemaphoreType.DMA((2,)),
         ],

time: 54 us -> 53.4 us (0.989)
    pallas_call x1, Pallas kernels: 53.1 us -> 52.6 us  [per_device(): pl.pallas_call(kernel, out_shape=pltpu.VMEM((2, ANGLES, BLOCK), jnp.bfloa...]
where the time goes in v6:
time: 53.4 us; the launch traced here: 53.3 us
  Pallas kernels  52.6 us (99%)
  local copies, waits for them, and re-layouts  0.71 us (1%)
    pallas_call x1, Pallas kernels, per_device(): pl.pallas_call(kernel, out_shape=pltpu.VMEM((2, ANGLES, BLOCK), jnp.bfloa...  52.6 us

profile of v6, /device:TPU:161, one launch (start us, length us, event | category | flops | bytes accessed | tf_op | source)
XLA Modules:
  0.0 53.3 jit_solution(11031805554197217066)
XLA Ops:
  0.0 52.6 %image_formation.1 = bf16[2,256,256]{2,1,0:T(8,128)(2,1)S(1)} custom-call(s32[8]{0:T(128)} %delays.1, bf16[2,128,8,128]{3,2,1,0:T(8,128)(2,1)} %bitcast.3, bf16[256,256]{1,0:T(8,128)(2,1)} %constant.12.clone.dft_in, bf16[2,144,256]{2,1,0:T(8,128)(2,1)} %constant.13.clone.dft_half_in, f32[2,128,128]{2,1,0:T(8,128)} %constant.14.clone.twiddle_in, ...), custom_call_target="tpu_custom_call" | custom-call | tf_op jit(solution)/shard_map/image_formation/pallas_call | solution.py:467
  52.6 0.7 %copy.10 = bf16[2,256,256]{2,1,0:T(8,128)(2,1)} copy(bf16[2,256,256]{2,1,0:T(8,128)(2,1)S(1)} %image_formation.1) | data formatting | bytes 524288

commit v7 on v6

--- a/solution.py
+++ b/solution.py
@@ -148,6 +148,7 @@
     outgoing,
     incoming,
     ready,
+    told,
     table_sem,
     plane_send,
     plane_recv,
@@ -159,6 +160,8 @@
     half = lax.div(gate, PEERS)
     peer = lax.rem(gate, PEERS)
     place = half * N_SUB + sub
+    core = lax.rem(peer, 2)
+    sibling = peer + 1 - 2 * core
     sector = swapped_bits(sub)
 
     loads = [
@@ -180,27 +183,41 @@
 
     barrier = pltpu.get_barrier_semaphore()
 
-    def at(spot):
-        return {"sub": lax.rem(spot, N_SUB), "gate": lax.div(spot, N_SUB) * PEERS + peer}
+    def at(spot, who=peer):
+        return {"sub": lax.rem(spot, N_SUB), "gate": lax.div(spot, N_SUB) * PEERS + who}
+
+    def signal(semaphore, to):
+        pl.semaphore_signal(semaphore, inc=1, device_id=to, device_id_type=MESH)
 
     def greet_plane(step, carry):
-        other = half * PEERS + lax.rem(peer + step, PEERS)
-        pl.semaphore_signal(barrier, inc=1, device_id={"gate": other}, device_id_type=MESH)
+        signal(barrier, at(place, lax.rem(peer - core + 2 * step, PEERS)))
         return carry
 
     def greet_ring(spot, carry):
-        pl.semaphore_signal(barrier, inc=1, device_id=at(spot), device_id_type=MESH)
+        signal(barrier, at(spot, peer - core + 1))
         return carry
 
     def answer_ring(spot, carry):
-        pl.semaphore_signal(ready.at[place], inc=1, device_id=at(spot), device_id_type=MESH)
+        signal(ready.at[place], at(spot, peer))
+        signal(ready.at[place], at(spot, sibling))
         return carry
 
-    lax.fori_loop(1, PEERS, greet_plane, 0)
+    def hear_ring():
+        pl.semaphore_wait(barrier, 2 * place + 1)
+        lax.fori_loop(0, place, answer_ring, 0)
+        signal(told, at(place, sibling))
+
+    signal(barrier, at(place, sibling))
     lax.fori_loop(place + 1, RING, greet_ring, 0)
+    lax.fori_loop(1, PEERS // 2, greet_plane, 0)
 
     for load in loads[:3]:
         load.wait()
+    prompt = place < N_SUB + N_SUB // 2
+
+    @pl.when((core == 1) & prompt)
+    def _():
+        hear_ring()
 
     for part in range(2):
         spread[part] = raw[part].astype(jnp.float32).reshape(RADIX * OWN, RADIX)
@@ -275,10 +292,11 @@
 
     def plane_starts(stage):
         def start(step, carry):
-            plane_copy(stage, step).start()
+            far_first = 1 + lax.rem(step + PEERS // 2 - 2, PEERS - 1)
+            plane_copy(stage, far_first).start()
             return carry
 
-        lax.fori_loop(1, PEERS, start, 0)
+        lax.fori_loop(0, PEERS - 1, start, 0)
         for chunk in (stage,) if stage < 2 else (0, 1):
             pulses[chunk, stage // 2, peer] = blocks[chunk, stage // 2, peer]
 
@@ -384,8 +402,20 @@
 
     loads[3].wait()
     range_gates(0)
-    pl.semaphore_wait(barrier, PEERS - 1 + place)
-    lax.fori_loop(0, place, answer_ring, 0)
+
+    @pl.when(core == 0)
+    def _():
+        pl.semaphore_wait(barrier, PEERS - 1)
+        signal(told, at(place, sibling))
+
+    @pl.when((core == 1) & jnp.logical_not(prompt))
+    def _():
+        hear_ring()
+
+    @pl.when(core == 1)
+    def _():
+        pl.semaphore_wait(told, 1)
+
     plane_starts(0)
     plane_starts(1)
     range_gates(1)
@@ -394,6 +424,12 @@
     for stage in range(STAGES):
         plane_wait(stage, plane_recv)
         beam_sums(stage)
+        if stage == 0:
+
+            @pl.when(core == 0)
+            def _():
+                pl.semaphore_wait(told, 1)
+
         ring_starts(stage)
     for load in loads[5:]:
         load.wait()
@@ -487,6 +523,7 @@
             pltpu.VMEM((RING * TILES, 8, RADIX), jnp.bfloat16),
             pltpu.VMEM((RING * TILES, 8, RADIX), jnp.bfloat16),
             pltpu.SemaphoreType.REGULAR((RING,)),
+            pltpu.SemaphoreType.REGULAR,
             pltpu.SemaphoreType.DMA((7,)),
             pltpu.SemaphoreType.DMA((STAGES,)),
             pltpu.SemaphoreType.DMA((STAGES,)),

time: 53.4 us -> 52.6 us (0.985)
  Pallas kernels: 52.6 us -> 51.8 us
    pallas_call x1, Pallas kernels: 52.6 us -> 51.8 us  [per_device(): pl.pallas_call(kernel, out_shape=pltpu.VMEM((2, ANGLES, BLOCK), jnp.bfloa...]
where the time goes in v7:
time: 52.6 us; the launch traced here: 52.5 us
  Pallas kernels  51.8 us (98%)
  local copies, waits for them, and re-layouts  0.71 us (1%)
    pallas_call x1, Pallas kernels, per_device(): pl.pallas_call(kernel, out_shape=pltpu.VMEM((2, ANGLES, BLOCK), jnp.bfloa...  51.8 us

profile of v7, /device:TPU:161, one launch (start us, length us, event | category | flops | bytes accessed | tf_op | source)
XLA Modules:
  0.0 52.5 jit_solution(8334212915207117860)
XLA Ops:
  0.0 51.8 %image_formation.1 = bf16[2,256,256]{2,1,0:T(8,128)(2,1)S(1)} custom-call(s32[8]{0:T(128)} %delays.1, bf16[2,128,8,128]{3,2,1,0:T(8,128)(2,1)} %bitcast.3, bf16[256,256]{1,0:T(8,128)(2,1)} %constant.12.clone.dft_in, bf16[2,144,256]{2,1,0:T(8,128)(2,1)} %constant.13.clone.dft_half_in, f32[2,128,128]{2,1,0:T(8,128)} %constant.14.clone.twiddle_in, ...), custom_call_target="tpu_custom_call" | custom-call | tf_op jit(solution)/shard_map/image_formation/pallas_call | solution.py:503
  51.8 0.7 %copy.10 = bf16[2,256,256]{2,1,0:T(8,128)(2,1)} copy(bf16[2,256,256]{2,1,0:T(8,128)(2,1)S(1)} %image_formation.1) | data formatting | bytes 524288

commit v8 on v7

--- a/solution.py
+++ b/solution.py
@@ -19,6 +19,7 @@
 PEERS = 32
 RING = HALVES * N_SUB
 STAGES = 3
+BATCH = 4
 OWN = 8
 BLOCK = 256
 WINDOW = 42
@@ -29,6 +30,7 @@
 FIRST_TILES = 10
 ALL_TILES = N_SUB * (TILES + EDGE_TILES)
 HELD = RADIX // HALVES + 8
+SECTORS = (0, 4, 2, 6, 1, 5, 3, 7)
 STARTS = (0, 26, 60, 90)
 WIDTHS = (EDGE_WINDOW, WINDOW, WINDOW, EDGE_WINDOW)
 TWO_PI = 2.0 * math.pi
@@ -67,7 +69,7 @@
     result = np.zeros((HALVES, N_SUB, ROWS, PEERS * 2 * OWN))
     for half in range(HALVES):
         pulses = half * PEERS * OWN + np.arange(PEERS * OWN)
-        for q in range(N_SUB):
+        for slot, q in enumerate(SECTORS):
             beams = 128 * (q // 4) + STARTS[q % 4] + np.arange(WIDTHS[q % 4])
             turns = (2 * beams[:, None] - ANGLES + 1) * (2 * pulses[None, :] - SUB_PULSES + 1)
             table = np.exp(-1j * TWO_PI / 4096 * (turns % 4096)) / math.sqrt(SUB_PULSES)
@@ -75,7 +77,7 @@
             upper = np.stack([table.real, -table.imag], axis=2)
             lower = np.stack([table.imag, table.real], axis=2)
             rows = np.stack([upper, lower], axis=1).reshape(-1, PEERS * 2 * OWN)
-            result[half, q, : len(rows)] = rows
+            result[half, slot, : len(rows)] = rows
     return bf16(result.reshape(HALVES, N_SUB * ROWS, PEERS * 2 * OWN))
 
 
@@ -308,19 +310,20 @@
             semaphores.at[stage],
         ).wait()
 
-    def beam_sums(stage):
+    def beam_sums(stage, batch):
         side = stage // 2
         chunks = (stage,) if stage < 2 else (0, 1)
         beams = jnp.dot(
-            steer[...],
+            steer[batch * BATCH * ROWS : (batch + 1) * BATCH * ROWS, :],
             jnp.concatenate(
                 [pulses[chunk, side].reshape(PEERS * 2 * OWN, RADIX) for chunk in chunks], axis=1
             ),
             preferred_element_type=jnp.float32,
         )
         for place_in, chunk in enumerate(chunks):
-            for q in range(N_SUB):
-                window = beams[q * ROWS : (q + 1) * ROWS, place_in * RADIX : (place_in + 1) * RADIX]
+            for slot in range(BATCH):
+                q = SECTORS[batch * BATCH + slot]
+                window = beams[slot * ROWS : (slot + 1) * ROWS, place_in * RADIX : (place_in + 1) * RADIX]
                 window = window.reshape(ROWS // 8, 8, RADIX)
                 shared = WIDTHS[q % 4] // 4
                 base = (side * N_SUB + q) * TILES + chunk * FIRST_TILES
@@ -368,7 +371,7 @@
         def _():
             act(large)
 
-    def ring_starts(stage):
+    def ring_starts(stage, batch):
         side = stage // 2
         chunks = (stage,) if stage < 2 else (0, 1)
 
@@ -392,13 +395,15 @@
                 pl.semaphore_wait(ready.at[spot], 1)
             return start(spot, carry)
 
-        first = side * N_SUB
-        lax.fori_loop(first, jnp.minimum(place, first + N_SUB), start, 0)
-        lax.fori_loop(jnp.maximum(place + 1, first), first + N_SUB, start_later, 0)
-
-        @pl.when(half == side)
-        def _():
-            act(sub, own_copy)
+        first = side * N_SUB + batch * BATCH
+        lax.fori_loop(first, jnp.minimum(place, first + BATCH), start, 0)
+        lax.fori_loop(jnp.maximum(place + 1, first), first + BATCH, start_later, 0)
+
+        if batch == 1:
+
+            @pl.when(half == side)
+            def _():
+                act(sub, own_copy)
 
     loads[3].wait()
     range_gates(0)
@@ -423,14 +428,15 @@
     loads[4].wait()
     for stage in range(STAGES):
         plane_wait(stage, plane_recv)
-        beam_sums(stage)
-        if stage == 0:
-
-            @pl.when(core == 0)
-            def _():
-                pl.semaphore_wait(told, 1)
-
-        ring_starts(stage)
+        for batch in range(N_SUB // BATCH):
+            beam_sums(stage, batch)
+            if stage == 0 and batch == 0:
+
+                @pl.when(core == 0)
+                def _():
+                    pl.semaphore_wait(told, 1)
+
+            ring_starts(stage, batch)
     for load in loads[5:]:
         load.wait()
 

time: 52.6 us -> 52.3 us (level)
  no operation moved by 1% of the time
where the time goes in v8:
time: 52.3 us; the launch traced here: 52.2 us
  Pallas kernels  51.5 us (98%)
  local copies, waits for them, and re-layouts  0.71 us (1%)
    pallas_call x1, Pallas kernels, per_device(): pl.pallas_call(kernel, out_shape=pltpu.VMEM((2, ANGLES, BLOCK), jnp.bfloa...  51.5 us

profile of v8, /device:TPU:161, one launch (start us, length us, event | category | flops | bytes accessed | tf_op | source)
XLA Modules:
  0.0 52.2 jit_solution(15678501279612689070)
XLA Ops:
  0.0 51.5 %image_formation.1 = bf16[2,256,256]{2,1,0:T(8,128)(2,1)S(1)} custom-call(s32[8]{0:T(128)} %delays.1, bf16[2,128,8,128]{3,2,1,0:T(8,128)(2,1)} %bitcast.3, bf16[256,256]{1,0:T(8,128)(2,1)} %constant.12.clone.dft_in, bf16[2,144,256]{2,1,0:T(8,128)(2,1)} %constant.13.clone.dft_half_in, f32[2,128,128]{2,1,0:T(8,128)} %constant.14.clone.twiddle_in, ...), custom_call_target="tpu_custom_call" | custom-call | tf_op jit(solution)/shard_map/image_formation/pallas_call | solution.py:509
  51.5 0.7 %copy.10 = bf16[2,256,256]{2,1,0:T(8,128)(2,1)} copy(bf16[2,256,256]{2,1,0:T(8,128)(2,1)S(1)} %image_formation.1) | data formatting | bytes 524288

commit v9 on v8

--- a/solution.py
+++ b/solution.py
@@ -397,9 +397,14 @@
 
         first = side * N_SUB + batch * BATCH
         lax.fori_loop(first, jnp.minimum(place, first + BATCH), start, 0)
-        lax.fori_loop(jnp.maximum(place + 1, first), first + BATCH, start_later, 0)
-
-        if batch == 1:
+        later = jnp.maximum(place + 1, first)
+        stop = first + BATCH
+        if stage == 2:
+            lax.fori_loop(later, stop, lambda i, c: start_later(later + stop - 1 - i, c), 0)
+        else:
+            lax.fori_loop(later, stop, start_later, 0)
+
+        if batch == (1 if stage < 2 else 0):
 
             @pl.when(half == side)
             def _():
@@ -428,7 +433,7 @@
     loads[4].wait()
     for stage in range(STAGES):
         plane_wait(stage, plane_recv)
-        for batch in range(N_SUB // BATCH):
+        for batch in (0, 1) if stage < 2 else (1, 0):
             beam_sums(stage, batch)
             if stage == 0 and batch == 0:
 

time: 52.3 us -> 52.3 us (level)
  no operation moved by 1% of the time
where the time goes in v9:
time: 52.3 us; the launch traced here: 52.2 us
  Pallas kernels  51.5 us (98%)
  local copies, waits for them, and re-layouts  0.71 us (1%)
    pallas_call x1, Pallas kernels, per_device(): pl.pallas_call(kernel, out_shape=pltpu.VMEM((2, ANGLES, BLOCK), jnp.bfloa...  51.5 us

profile of v9, /device:TPU:161, one launch (start us, length us, event | category | flops | bytes accessed | tf_op | source)
XLA Modules:
  0.0 52.2 jit_solution(4487619168209735844)
XLA Ops:
  0.0 51.5 %image_formation.1 = bf16[2,256,256]{2,1,0:T(8,128)(2,1)S(1)} custom-call(s32[8]{0:T(128)} %delays.1, bf16[2,128,8,128]{3,2,1,0:T(8,128)(2,1)} %bitcast.3, bf16[256,256]{1,0:T(8,128)(2,1)} %constant.12.clone.dft_in, bf16[2,144,256]{2,1,0:T(8,128)(2,1)} %constant.13.clone.dft_half_in, f32[2,128,128]{2,1,0:T(8,128)} %constant.14.clone.twiddle_in, ...), custom_call_target="tpu_custom_call" | custom-call | tf_op jit(solution)/shard_map/image_formation/pallas_call | solution.py:514
  51.5 0.7 %copy.10 = bf16[2,256,256]{2,1,0:T(8,128)(2,1)} copy(bf16[2,256,256]{2,1,0:T(8,128)(2,1)S(1)} %image_formation.1) | data formatting | bytes 524288
